TPU v7x, 32 devices: a whole 2x2x4 slice. The times are simulated.
32 devices in a mesh: facet: 4 (over z), strip: 8 (over y, x, core).
Axes of the slice: x: 2, y: 2, z: 4, core: 2. Of those that a mesh axis runs over, the one named last changes fastest.
Arguments:
- sky_components: bfloat16 [4, 2, 4, 2048, 2048], P('facet', None, None, 'strip'), may hold values from -6 to 6
- scale_kernels: float32 [4, 33], replicated, may hold values from 0.026111647 to 0.26111647
- row_taper: bfloat16 [4, 2048, 512], P('facet'), may hold values from -0.125 to 0.125
- col_taper: bfloat16 [4, 2048, 1024], P('facet'), may hold values from -0.125 to 0.125
- finish_rows: bfloat16 [4, 512, 128], replicated, may hold values from -0.25 to 0.25
- finish_cols: bfloat16 [4, 512, 128], replicated, may hold values from -0.5 to 0.5
- subgrid_owner: int32 [32], replicated, may hold values from 0 to 31, as said below
- block_cell: int32 [2048, 2], P(('facet', 'strip')), may hold values from 0 to 480
- vis_offset: float32 [2048, 2, 128], P(('facet', 'strip')), may hold values from 0 to 31
- block_owner: int32 [2048, 1], P(('facet', 'strip')), may hold values from 0 to 31; in each aligned block of 64 rows (0 to 63, 64 to 127, ...) at most 4 rows name the same one
- observed: float32 [4096, 2, 128], P(('facet', 'strip')), may hold values from -6 to 6
- antenna_pair_index: int32 [4096, 2, 128], P(('facet', 'strip')), may hold values from 0 to 511
- gains: float32 [2, 512], replicated, may hold values from 0.1 to 1.9
Outputs:
- subgrids: bfloat16 [32, 2, 512, 512], P(('facet', 'strip'))
- residual: float32 [4096, 2, 128], P(('facet', 'strip'))
Inputs may be any that keep to these rules, and one draw needn't show every extreme that they name: Every device number appears once; subgrid_owner[a * 8 + b] = rowperm(a) * 8 + colperm(b) for a permutation rowperm of the subgrid rows and a permutation colperm of the subgrid columns. `block_owner`: among the 64 blocks of one device at most 4 share an owner, and some owner takes exactly 4 of them.
All inputs are finite; a program needn't handle non-finite values.
Results may differ from a plain program's by a relative error of at most 0.02.
Values may be sent and summed in bfloat16 or wider, within the bound.
A program may use at most 128 MiB of HBM per device.

v0:
```python
import jax
import jax.numpy as jnp
from jax import lax
from jax.sharding import PartitionSpec as P

TILE = 32


KERNEL_WIDTH = 1.5


def extended(x, sides, width):
    for axis, dim in sides:
        count, length = (lax.axis_size(axis), x.shape[dim])
        up = [(i, (i + 1) % count) for i in range(count - 1)]
        down = [(j, i) for i, j in up]
        last = lax.slice_in_dim(x, length - width, length, axis=dim)
        initial = lax.slice_in_dim(x, 0, width, axis=dim)
        before = lax.ppermute(last, axis, up)
        after = lax.ppermute(initial, axis, down)
        x = jnp.concatenate([before, x, after], axis=dim)
    return x


def smooth_rows_cols(padded, kernels, rows):
    taps = kernels.shape[1]
    width = (taps - 1) // 2
    along_rows = jnp.zeros(padded.shape[:2] + (rows, padded.shape[3]), jnp.float32)
    for tap in range(taps):
        along_rows = along_rows + kernels[:, tap][None, :, None, None] * padded[
            :, :, tap : tap + rows, :
        ].astype(jnp.float32)
    cols = along_rows.shape[3]
    wide = jnp.pad(along_rows, ((0, 0), (0, 0), (0, 0), (width, width)))
    total = jnp.zeros_like(along_rows)
    for tap in range(taps):
        total = total + kernels[:, tap][None, :, None, None] * wide[:, :, :, tap : tap + cols]
    return jnp.sum(total, axis=1).astype(jnp.bfloat16)


def window_weights(corner, offset, grid_side, tile_side):
    places = jnp.arange(grid_side, dtype=jnp.int32)
    relative = places[None, :] - corner[:, None]
    inside = (relative >= 0) & (relative < tile_side)
    delta = (relative.astype(jnp.float32)[:, None, :] - offset[:, :, None]) / KERNEL_WIDTH
    return jnp.where(inside[:, None, :], jnp.exp(-0.5 * delta * delta), 0.0)


def inverse_of(perm):
    count = perm.shape[0]
    places = jnp.arange(count, dtype=jnp.int32)
    return jnp.sum(jnp.where(perm[None, :] == places[:, None], places[None, :], 0), axis=1)


def on_device(
    sky_components,
    scale_kernels,
    row_taper,
    col_taper,
    finish_rows,
    finish_cols,
    subgrid_owner,
    block_cell,
    vis_offset,
    block_owner,
    observed,
    antenna_pair_index,
    gains,
):
    n_facet = lax.axis_size("facet")
    n_strip = lax.axis_size("strip")
    devices = n_facet * n_strip
    comp = sky_components[0]
    corr = comp.shape[0]
    rows = comp.shape[2]
    facet_side = comp.shape[3]
    contrib_side = finish_cols.shape[2]
    grid_side = finish_cols.shape[1]
    sub_rows = row_taper.shape[2] // contrib_side
    sub_cols = col_taper.shape[2] // contrib_side
    width = (scale_kernels.shape[1] - 1) // 2
    tile_side = TILE
    padded = extended(comp, (("strip", 2),), width)
    smoothed = smooth_rows_cols(padded, scale_kernels, rows)
    col_products = jnp.einsum(
        "crw,wk->crk", smoothed, col_taper[0], preferred_element_type=jnp.float32
    ).astype(jnp.bfloat16)
    col_products = col_products.reshape(corr, rows, sub_cols, contrib_side)
    col_perm = subgrid_owner[:sub_cols] % n_strip
    row_perm = subgrid_owner[jnp.arange(sub_rows, dtype=jnp.int32) * sub_cols] // n_strip
    col_inverse = inverse_of(col_perm)
    row_inverse = inverse_of(row_perm)
    by_target = jnp.take(col_products, col_inverse, axis=2)
    regrouped = lax.all_to_all(by_target, "strip", split_axis=2, concat_axis=1, tiled=True)
    all_rows = row_taper[0].reshape(facet_side, sub_rows, contrib_side)
    finished = jnp.einsum(
        "rai,crj->acij", all_rows, regrouped[:, :, 0, :], preferred_element_type=jnp.float32
    ).astype(jnp.bfloat16)
    outgoing = jnp.take(finished, row_inverse, axis=0)
    mine = lax.all_to_all(outgoing, "facet", split_axis=0, concat_axis=0, tiled=True)
    spread = jnp.einsum(
        "fcij,fsj->fcis", mine, finish_cols, preferred_element_type=jnp.float32
    ).astype(jnp.bfloat16)
    subgrid = jnp.einsum(
        "fri,fcis->crs", finish_rows, spread, preferred_element_type=jnp.float32
    ).astype(jnp.bfloat16)
    blocks = block_owner.shape[0]
    group = min(blocks, 32)
    visibility_block = observed.shape[2]

    def predict_group(pieces):
        cells, offsets = pieces
        row_weights = window_weights(cells[:, 0], offsets[:, 0, :], grid_side, tile_side).astype(
            jnp.bfloat16
        )
        col_weights = window_weights(cells[:, 1], offsets[:, 1, :], grid_side, tile_side)
        along = jnp.einsum(
            "kvx,cxy->kcvy", row_weights, subgrid, preferred_element_type=jnp.float32
        )
        return jnp.sum(along * col_weights[:, None, :, :], axis=3)

    grouped_cells = block_cell.reshape(blocks // group, group, 2)
    grouped_offsets = vis_offset.reshape(blocks // group, group, 2, visibility_block)
    predicted = lax.map(predict_group, (grouped_cells, grouped_offsets)).reshape(
        blocks, corr * visibility_block
    )
    dest = block_owner[:, 0]
    same = dest[:, None] == dest[None, :]
    order = jnp.arange(blocks, dtype=jnp.int32)
    earlier = order[None, :] < order[:, None]
    rank = jnp.sum((same & earlier).astype(jnp.int32), axis=1)
    capacity = observed.shape[0] // devices
    target = dest * capacity + rank
    slots = jnp.arange(devices * capacity, dtype=jnp.int32)
    placing = (slots[:, None] == target[None, :]).astype(jnp.float32)
    outgoing_vis = jnp.dot(
        placing, predicted, precision=lax.Precision.HIGHEST, preferred_element_type=jnp.float32
    )
    outgoing_vis = outgoing_vis.reshape(devices, capacity, corr, visibility_block)
    arrived = lax.all_to_all(
        outgoing_vis.astype(jnp.bfloat16),
        ("facet", "strip"),
        split_axis=0,
        concat_axis=0,
        tiled=True,
    ).astype(outgoing_vis.dtype)
    placed = arrived.reshape(devices * capacity, corr, visibility_block)
    gain_p = jnp.take(gains, antenna_pair_index[:, 0, :], axis=1)
    gain_q = jnp.take(gains, antenna_pair_index[:, 1, :], axis=1)
    product = jnp.transpose(gain_p * gain_q, (1, 0, 2))
    residual = observed - product * placed
    return (subgrid[None], residual)


def solution(mesh):
    placed = (
        P("facet", None, None, "strip", None),
        P(),
        P("facet", None, None),
        P("facet", None, None),
        P(),
        P(),
        P(),
        P(("facet", "strip"), None),
        P(("facet", "strip"), None, None),
        P(("facet", "strip"), None),
        P(("facet", "strip"), None, None),
        P(("facet", "strip"), None, None),
        P(),
    )
    return jax.shard_map(
        on_device,
        mesh=mesh,
        in_specs=placed,
        out_specs=(P(("facet", "strip"), None, None, None), P(("facet", "strip"), None, None)),
        check_vma=False,
    )
```

profile of v0, /device:TPU:0, one launch (start us, length us, event | category | flops | bytes accessed | tf_op | source)
XLA Modules:
  0.0 665.4 jit_solution(11906201447690767586)
XLA Ops:
  0.6 0.0 copy-start
  0.6 1.3 fusion.123
  2.0 2.4 collective-permute-start
  4.4 1.3 collective-permute-start.1
  5.7 1.9 slice_reduce_fusion.32
  7.6 1.6 slice_reduce_fusion.31
  9.2 0.7 and_select_fusion
  9.9 0.1 select_reduce_fusion
  10.1 1.3 gather_fusion
  11.4 0.1 select_reduce_fusion.1
  11.5 1.1 fusion.124
  12.6 0.0 collective-permute-done
  12.6 0.0 collective-permute-done.1
  12.6 136.0 %multiply_add_fusion = f32[2,4,256,2048]{3,2,1,0:T(8,128)} fusion(bf16[2,4,256,2048]{3,2,1,0:T(8,128)(2,1)} %bitcast.137, bf16[2,4,16,2048]{3,2,1,0:T(8,128)(2,1)S(1)} %collective-permute-done.1, bf16[2,4,16,2048]{3,2,1,0:T(8,128)(2,1)S(1)} %collective-permute-done, f32[4]{0:T(128)S(1)} %get-tuple-element.158, f32[4]{0:T(128)S(1)} %get-tuple-element.159, ...), kind=kLoop, calls=%fused_computation.121 | loop fusion | flops 813694976 | bytes 26214928 | tf_op jit(solution)/shard_map/add | solution.py:30
  148.6 0.0 copy-start.6
  148.6 324.8 %add_reduce_fusion = bf16[2,256,2048]{2,1,0:T(8,128)(2,1)S(1)} fusion(f32[2,4,256,2048]{3,2,1,0:T(8,128)} %multiply_add_fusion, f32[4]{0:T(128)S(1)} %get-tuple-element.158, f32[4]{0:T(128)S(1)} %get-tuple-element.159, f32[4]{0:T(128)S(1)} %get-tuple-element.128, f32[4]{0:T(128)S(1)} %get-tuple-element.129, f32[4]{0:T(128)S(1)} %get-tuple-element.130, ...), kind=kLoop, calls=%fused_computation.76 | loop fusion | flops 275775488 | bytes 18874896 | tf_op jit(solution)/shard_map/reduce_sum | solution.py:38
  473.5 0.0 copy-start.5
  473.5 0.0 copy-start.4
  473.5 2.3 fusion.96
  475.8 0.2 copy.159
  476.1 0.7 gather_fusion.1
  476.8 1.1 select_bitcast_fusion
  478.0 10.0 %all-to-all-start = ((bf16[2,256,8,128]{3,1,0,2:T(8,128)(2,1)}), bf16[2,256,8,128]{3,1,0,2:T(8,128)(2,1)S(1)}, u32[]{:S(2)}, u32[]{:S(2)}) async-start(bf16[2,256,8,128]{3,1,0,2:T(8,128)(2,1)} %select_bitcast_fusion), calls=%async_computation | async-start | bytes 2097152 | tf_op jit(solution)/shard_map/all_to_all | solution.py:94
  488.0 0.0 copy-start.8
  488.0 0.0 copy-start.7
  488.0 4.0 reshape_squeeze.3
  492.1 11.3 %all-to-all-done = bf16[2,256,8,128]{3,1,0,2:T(8,128)(2,1)S(1)} async-done(((bf16[2,256,8,128]{3,1,0,2:T(8,128)(2,1)}), bf16[2,256,8,128]{3,1,0,2:T(8,128)(2,1)S(1)}, u32[]{:S(2)}, u32[]{:S(2)}) %all-to-all-start) | async-done | bytes 1048608 | tf_op jit(solution)/shard_map/all_to_all | solution.py:94
  503.4 0.1 copy.101
  503.5 2.3 fusion.104
  505.8 0.2 copy.104
  506.0 0.6 gather_fusion.2
  506.6 0.8 broadcast_select_fusion
  507.4 4.9 all-to-all-start.1
  512.3 0.0 copy-done.5
  512.3 0.1 reshape.259
  512.4 0.0 copy-done.4
  512.4 0.1 copy.107
  512.5 54.4 %gather_fusion.3 = f32[16384,2]{1,0:T(8,128)} fusion(f32[2,512]{0,1:T(8,128)S(1)} %copy.107, s32[16384]{0:T(1024)S(1)} %bitcast_clamp_fusion.1), kind=kCustom, calls=%fused_computation.clone | custom fusion | bytes 327680 | tf_op jit(solution)/shard_map/jit(_take)/gather | solution.py:148
  566.9 5.2 copy.108
  572.2 54.4 %gather_fusion.4 = f32[16384,2]{1,0:T(8,128)} fusion(f32[2,512]{0,1:T(8,128)S(1)} %copy.107, s32[16384]{0:T(1024)S(1)} %bitcast_clamp_fusion), kind=kCustom, calls=%fused_computation.1.clone | custom fusion | bytes 327680 | tf_op jit(solution)/shard_map/jit(_take)/gather | solution.py:149
  626.6 5.2 copy.110
  631.8 0.0 copy-done.8
  631.8 0.2 convert_reduce_fusion
  632.0 0.0 all-to-all-done.1
  632.0 1.0 bitcast_convert_fusion
  633.0 0.5 copy.114
  633.6 0.0 copy-start.3
  633.6 17.7 %while.13 = (s32[]{:T(128)}, f32[2,32,2,128]{3,2,1,0:T(2,128)S(1)}, s32[2,32,2]{1,0,2:T(2,128)S(1)}, f32[2,32,2,128]{3,2,1,0:T(2,128)S(1)}, bf16[2,512,512]{2,1,0:T(8,128)(2,1)S(1)}, /*index=5*/s32[]{:T(128)}) while((s32[]{:T(128)}, f32[2,32,2,128]{3,2,1,0:T(2,128)S(1)}, s32[2,32,2]{1,0,2:T(2,128)S(1)}, f32[2,32,2,128]{3,2,1,0:T(2,128)S(1)}, ...), condition=%wide.region_6.8_spmd, body=%wide.region_4.7_spmd.sunk | while | flops 4326612992 | bytes 18482768 | solution.py:124
  633.6 0.1 fusion.134
  633.7 0.1 fusion.135
  633.9 2.6 fusion.136
  636.5 6.0 multiply_reduce_fusion.2
  642.5 0.1 fusion.134
  642.6 0.1 fusion.135
  642.7 2.6 fusion.136
  645.3 6.0 multiply_reduce_fusion.2
  651.3 0.0 copy-start.1
  651.3 0.3 convolution_convert_fusion.1
  651.6 0.7 copy.116
  652.3 4.7 all-to-all-start.2
  657.1 1.3 copy.120
  658.4 6.0 all-to-all-done.2
  664.4 0.1 copy.118
  664.6 0.8 copy.121
  (36 shorter events, 0.3 us)
Async XLA Ops:
  0.6 631.4 %copy-start = (bf16[4,512,128]{2,1,0:T(8,128)(2,1)S(1)}, bf16[4,512,128]{2,1,0:T(8,128)(2,1)}, u32[]{:S(2)}) copy-start(bf16[4,512,128]{2,1,0:T(8,128)(2,1)} %param.21) | copy-start | bytes 1572868
  2.0 10.6 %collective-permute-start = (bf16[2,4,16,2048]{3,2,1,0:T(8,128)(2,1)S(1)}, bf16[2,4,16,2048]{3,2,1,0:T(8,128)(2,1)S(1)}, u32[]{:S(2)}, u32[]{:S(2)}) collective-permute-start(bf16[2,4,16,2048]{3,2,1,0:T(8,128)(2,1)S(1)} %get-tuple-element.178), channel_id=1, source_target_pairs={{0,1},{1,2},{2,3},{3,4},{4,5},{5,6},{6,7},{8,9},{9,10},{10,11},{11... | collective-permute-start | bytes 1572872 | tf_op jit(solution)/shard_map/ppermute | solution.py:19
  4.4 8.2 %collective-permute-start.1 = (bf16[2,4,16,2048]{3,2,1,0:T(8,128)(2,1)S(1)}, bf16[2,4,16,2048]{3,2,1,0:T(8,128)(2,1)S(1)}, u32[]{:S(2)}, u32[]{:S(2)}) collective-permute-start(bf16[2,4,16,2048]{3,2,1,0:T(8,128)(2,1)S(1)} %get-tuple-element.179), channel_id=1, source_target_pairs={{1,0},{2,1},{3,2},{4,3},{5,4},{6,5},{7,6},{9,8},{10,9},{11,10},{12... | collective-permute-start | bytes 1572872 | tf_op jit(solution)/shard_map/ppermute | solution.py:20
  148.6 324.8 %copy-start.6 = (bf16[1,2048,1024]{2,1,0:T(8,128)(2,1)S(1)}, bf16[1,2048,1024]{2,1,0:T(8,128)(2,1)}, u32[]{:S(2)}) copy-start(bf16[1,2048,1024]{2,1,0:T(8,128)(2,1)} %param.20) | copy-start | bytes 12582916
  473.5 38.8 %copy-start.5 = (s32[64,2]{0,1:T(2,128)S(1)}, s32[64,2]{0,1:T(2,128)}, u32[]{:S(2)}) copy-start(s32[64,2]{0,1:T(2,128)} %param.24) | copy-start | bytes 1540
  473.5 38.9 %copy-start.4 = (f32[2,512]{1,0:T(2,128)S(1)}, f32[2,512]{1,0:T(2,128)}, u32[]{:S(2)}) copy-start(f32[2,512]{1,0:T(2,128)} %param.29) | copy-start | bytes 12292
  478.0 25.4 %all-to-all-start = ((bf16[2,256,8,128]{3,1,0,2:T(8,128)(2,1)}), bf16[2,256,8,128]{3,1,0,2:T(8,128)(2,1)S(1)}, u32[]{:S(2)}, u32[]{:S(2)}) async-start(bf16[2,256,8,128]{3,1,0,2:T(8,128)(2,1)} %select_bitcast_fusion), calls=%async_computation | async-start | bytes 2097152 | tf_op jit(solution)/shard_map/all_to_all | solution.py:94
  488.0 143.8 %copy-start.8 = (s32[64,1]{0,1:T(1,128)S(1)}, s32[64,1]{0,1:T(1,128)}, u32[]{:S(2)}) copy-start(s32[64,1]{0,1:T(1,128)} %param.26) | copy-start | bytes 772
  488.0 144.0 %copy-start.7 = (bf16[4,512,128]{2,1,0:T(8,128)(2,1)S(1)}, bf16[4,512,128]{2,1,0:T(8,128)(2,1)}, u32[]{:S(2)}) copy-start(bf16[4,512,128]{2,1,0:T(8,128)(2,1)} %param.22) | copy-start | bytes 1572868
  503.4 130.2 %copy-start.2 = (f32[64,2,128]{2,1,0:T(2,128)S(1)}, f32[64,2,128]{2,1,0:T(2,128)}, u32[]{:S(2)}) copy-start(f32[64,2,128]{2,1,0:T(2,128)} %param.25) | copy-start | bytes 196612
  507.4 124.6 %all-to-all-start.1 = ((bf16[4,2,128,128]{3,2,1,0:T(8,128)(2,1)}), bf16[4,2,128,128]{3,2,1,0:T(8,128)(2,1)S(1)}, u32[]{:S(2)}, u32[]{:S(2)}) async-start(bf16[4,2,128,128]{3,2,1,0:T(8,128)(2,1)} %broadcast_select_fusion), calls=%async_computation.1 | async-start | bytes 524288 | tf_op jit(solution)/shard_map/all_to_all | solution.py:100
  633.6 31.0 %copy-start.3 = (f32[128,2,128]{2,1,0:T(2,128)S(1)}, f32[128,2,128]{2,1,0:T(2,128)}, u32[]{:S(2)}) copy-start(f32[128,2,128]{2,1,0:T(2,128)} %param.27) | copy-start | bytes 393220
  651.3 14.1 %copy-start.1 = (bf16[4,512,128]{2,1,0:T(8,128)(2,1)S(1)}, bf16[4,512,128]{2,1,0:T(8,128)(2,1)}, u32[]{:S(2)}) copy-start(bf16[4,512,128]{2,1,0:T(8,128)(2,1)} %param.21) | copy-start | bytes 1572868
  652.3 12.2 %all-to-all-start.2 = ((bf16[32,4,2,128]{3,2,1,0:T(2,128)(2,1)}), bf16[32,4,2,128]{3,2,1,0:T(2,128)(2,1)S(1)}, u32[]{:S(2)}, u32[]{:S(2)}) async-start(bf16[32,4,2,128]{3,2,1,0:T(2,128)(2,1)} %copy.116), calls=%async_computation.2 | async-start | bytes 131072 | tf_op jit(solution)/shard_map/all_to_all | solution.py:140
where the time goes:
time: 666 us; the launch traced here: 665 us
  other arithmetic  470 us (71%)
  local copies, waits for them, and re-layouts  136 us (20%)
  starting transfers between devices  23.4 us (4%)
  matrix products  17.8 us (3%)
  waiting for transfers between devices  17.3 us (3%)
    reduce_sum x1, other arithmetic, smooth_rows_cols(): return jnp.sum(total, axis=1).astype(jnp.bfloat16)  325 us
    add x1, other arithmetic, smooth_rows_cols(): along_rows + kernels[:, tap][None, :, None, None] * padded[:, :, tap:tap...  136 us
    gather x2, local copies, waits for them, and re-layouts, on_device(): gain_q = jnp.take(gains, antenna_pair_index[:, 1, :], axis=1)  59.6 us
    gather x2, local copies, waits for them, and re-layouts, on_device(): gain_p = jnp.take(gains, antenna_pair_index[:, 0, :], axis=1)  59.6 us
  transfers between devices with their start and end apart: 5, of which 2 were waited for; matrix products, arithmetic and copies ran while one was open for 20% of the time, Pallas kernels for 0%

commit v1 on v0

--- a/solution.py
+++ b/solution.py
@@ -1,6 +1,8 @@
 import jax
 import jax.numpy as jnp
 from jax import lax
+from jax.experimental import pallas as pl
+from jax.experimental.pallas import tpu as pltpu
 from jax.sharding import PartitionSpec as P
 
 TILE = 32
@@ -9,33 +11,164 @@
 KERNEL_WIDTH = 1.5
 
 
-def extended(x, sides, width):
-    for axis, dim in sides:
-        count, length = (lax.axis_size(axis), x.shape[dim])
-        up = [(i, (i + 1) % count) for i in range(count - 1)]
-        down = [(j, i) for i, j in up]
-        last = lax.slice_in_dim(x, length - width, length, axis=dim)
-        initial = lax.slice_in_dim(x, 0, width, axis=dim)
-        before = lax.ppermute(last, axis, up)
-        after = lax.ppermute(initial, axis, down)
-        x = jnp.concatenate([before, x, after], axis=dim)
-    return x
-
-
-def smooth_rows_cols(padded, kernels, rows):
+LANES = 128
+COL_TILE = 256
+
+
+def halo_rows(x, axis, dim, width):
+    count, length = (lax.axis_size(axis), x.shape[dim])
+    up = [(i, (i + 1) % count) for i in range(count - 1)]
+    down = [(j, i) for i, j in up]
+    last = lax.slice_in_dim(x, length - width, length, axis=dim)
+    initial = lax.slice_in_dim(x, 0, width, axis=dim)
+    return lax.ppermute(last, axis, up), lax.ppermute(initial, axis, down)
+
+
+def band_matrices(kernels):
     taps = kernels.shape[1]
     width = (taps - 1) // 2
-    along_rows = jnp.zeros(padded.shape[:2] + (rows, padded.shape[3]), jnp.float32)
-    for tap in range(taps):
-        along_rows = along_rows + kernels[:, tap][None, :, None, None] * padded[
-            :, :, tap : tap + rows, :
-        ].astype(jnp.float32)
-    cols = along_rows.shape[3]
-    wide = jnp.pad(along_rows, ((0, 0), (0, 0), (0, 0), (width, width)))
-    total = jnp.zeros_like(along_rows)
-    for tap in range(taps):
-        total = total + kernels[:, tap][None, :, None, None] * wide[:, :, :, tap : tap + cols]
-    return jnp.sum(total, axis=1).astype(jnp.bfloat16)
+    span = LANES + taps - 1
+    k = lax.broadcasted_iota(jnp.int32, (span, LANES), 0)
+    n = lax.broadcasted_iota(jnp.int32, (span, LANES), 1)
+    i = lax.broadcasted_iota(jnp.int32, (LANES, span), 0)
+    m = lax.broadcasted_iota(jnp.int32, (LANES, span), 1)
+    down = jnp.zeros((kernels.shape[0], span, LANES), jnp.float32)
+    across = jnp.zeros((kernels.shape[0], LANES, span), jnp.float32)
+    for t in range(taps):
+        tap = kernels[:, t][:, None, None]
+        down = jnp.where((k - n == t)[None], tap, down)
+        across = jnp.where((m - i == t)[None], tap, across)
+    down, across = down.astype(jnp.bfloat16), across.astype(jnp.bfloat16)
+    tiles = COL_TILE // LANES
+    window = COL_TILE + 2 * LANES
+    pieces = []
+    for tile in range(tiles):
+        start = LANES - width + tile * LANES
+        pieces.append(jnp.pad(down, ((0, 0), (start, window - start - span), (0, 0))))
+    return across, jnp.concatenate(pieces, axis=2)
+
+
+def smooth_kernel(order_ref, x_ref, before_ref, after_ref, rows_ref, cols_ref, taper_ref, out_ref, y_ref, acc_ref):
+    step = pl.program_id(0)
+    tiles = pl.num_programs(0) - 1
+    corr, scales, rows = x_ref.shape[0], x_ref.shape[1], x_ref.shape[2]
+    width = before_ref.shape[2]
+    targets = out_ref.shape[0]
+
+    @pl.when(step == 0)
+    def _():
+        y_ref[:, :, 0:COL_TILE] = jnp.zeros((scales, corr * rows, COL_TILE), y_ref.dtype)
+        acc_ref[...] = jnp.zeros_like(acc_ref)
+
+    lane = pl.multiple_of((step + 1) * COL_TILE, COL_TILE)
+
+    @pl.when(step == tiles)
+    def _():
+        y_ref[:, :, pl.ds(lane, COL_TILE)] = jnp.zeros((scales, corr * rows, COL_TILE), y_ref.dtype)
+
+    @pl.when(step < tiles)
+    def _():
+        for c in range(corr):
+            for s in range(scales):
+                full = jnp.concatenate([before_ref[c, s], x_ref[c, s], after_ref[c, s]], axis=0)
+                for b in range(rows // LANES):
+                    part = full[b * LANES : (b + 1) * LANES + 2 * width]
+                    y = jnp.dot(rows_ref[s], part, preferred_element_type=jnp.float32)
+                    at = c * rows + b * LANES
+                    y_ref[s, at : at + LANES, pl.ds(lane, COL_TILE)] = y.astype(y_ref.dtype)
+
+    @pl.when(step > 0)
+    def _():
+        first = pl.multiple_of(step * COL_TILE - LANES, LANES)
+        smoothed = jnp.zeros((corr * rows, COL_TILE), jnp.float32)
+        for s in range(scales):
+            smoothed += jnp.dot(
+                y_ref[s, :, pl.ds(first, COL_TILE + 2 * LANES)],
+                cols_ref[s],
+                preferred_element_type=jnp.float32,
+            )
+        acc_ref[...] += jnp.dot(
+            smoothed.astype(jnp.bfloat16), taper_ref[...], preferred_element_type=jnp.float32
+        )
+
+    @pl.when(step == tiles)
+    def _():
+        for d in range(targets):
+            at = pl.multiple_of(order_ref[d] * LANES, LANES)
+            for c in range(corr):
+                out_ref[d, c] = acc_ref[c * rows : (c + 1) * rows, pl.ds(at, LANES)].astype(out_ref.dtype)
+
+
+def column_products(comp, before, after, kernels, taper, order):
+    corr, scales, rows, side = comp.shape
+    width = before.shape[2]
+    across, down = band_matrices(kernels)
+    tiles = side // COL_TILE
+    wide = taper.shape[1]
+    targets = wide // LANES
+    last = tiles - 1
+
+    def ahead(j, order):
+        return (0, 0, 0, jnp.minimum(j, last))
+
+    return pl.pallas_call(
+        smooth_kernel,
+        grid_spec=pltpu.PrefetchScalarGridSpec(
+            num_scalar_prefetch=1,
+            grid=(tiles + 1,),
+            in_specs=[
+                pl.BlockSpec((corr, scales, rows, COL_TILE), ahead),
+                pl.BlockSpec((corr, scales, width, COL_TILE), ahead),
+                pl.BlockSpec((corr, scales, width, COL_TILE), ahead),
+                pl.BlockSpec(across.shape, lambda j, order: (0, 0, 0)),
+                pl.BlockSpec(down.shape, lambda j, order: (0, 0, 0)),
+                pl.BlockSpec((COL_TILE, wide), lambda j, order: (jnp.maximum(j - 1, 0), 0)),
+            ],
+            out_specs=pl.BlockSpec((targets, corr, rows, LANES), lambda j, order: (0, 0, 0, 0)),
+            scratch_shapes=[
+                pltpu.VMEM((scales, corr * rows, side + 2 * COL_TILE), jnp.bfloat16),
+                pltpu.VMEM((corr * rows, wide), jnp.float32),
+            ],
+        ),
+        out_shape=jax.ShapeDtypeStruct((targets, corr, rows, LANES), jnp.bfloat16),
+        compiler_params=pltpu.CompilerParams(
+            dimension_semantics=("arbitrary",), vmem_limit_bytes=60 * 1024 * 1024
+        ),
+        name="column_products",
+    )(order, comp, before, after, across, down, taper)
+
+
+def looked_up(row, index):
+    low, high = index % LANES, index // LANES
+    out = None
+    for chunk in range(row.shape[1] // LANES):
+        table = jnp.broadcast_to(row[:, chunk * LANES : (chunk + 1) * LANES], index.shape)
+        got = jnp.take_along_axis(table, low, axis=1, mode="promise_in_bounds")
+        out = got if out is None else jnp.where(high == chunk, got, out)
+    return out
+
+
+def gain_kernel(gains_ref, index_ref, out_ref):
+    p, q = index_ref[:, 0, :], index_ref[:, 1, :]
+    for c in range(gains_ref.shape[0]):
+        row = gains_ref[c : c + 1, :]
+        out_ref[:, c, :] = looked_up(row, p) * looked_up(row, q)
+
+
+def gain_products(gains, index):
+    rows = index.shape[0]
+    step = min(rows, 128)
+    return pl.pallas_call(
+        gain_kernel,
+        grid=(rows // step,),
+        in_specs=[
+            pl.BlockSpec(gains.shape, lambda j: (0, 0)),
+            pl.BlockSpec((step,) + index.shape[1:], lambda j: (j, 0, 0)),
+        ],
+        out_specs=pl.BlockSpec((step, gains.shape[0], index.shape[2]), lambda j: (j, 0, 0)),
+        out_shape=jax.ShapeDtypeStruct((rows, gains.shape[0], index.shape[2]), jnp.float32),
+        name="gain_products",
+    )(gains, index)
 
 
 def window_weights(corner, offset, grid_side, tile_side):
@@ -80,21 +213,16 @@
     sub_cols = col_taper.shape[2] // contrib_side
     width = (scale_kernels.shape[1] - 1) // 2
     tile_side = TILE
-    padded = extended(comp, (("strip", 2),), width)
-    smoothed = smooth_rows_cols(padded, scale_kernels, rows)
-    col_products = jnp.einsum(
-        "crw,wk->crk", smoothed, col_taper[0], preferred_element_type=jnp.float32
-    ).astype(jnp.bfloat16)
-    col_products = col_products.reshape(corr, rows, sub_cols, contrib_side)
+    before, after = halo_rows(comp, "strip", 2, width)
     col_perm = subgrid_owner[:sub_cols] % n_strip
     row_perm = subgrid_owner[jnp.arange(sub_rows, dtype=jnp.int32) * sub_cols] // n_strip
     col_inverse = inverse_of(col_perm)
     row_inverse = inverse_of(row_perm)
-    by_target = jnp.take(col_products, col_inverse, axis=2)
-    regrouped = lax.all_to_all(by_target, "strip", split_axis=2, concat_axis=1, tiled=True)
-    all_rows = row_taper[0].reshape(facet_side, sub_rows, contrib_side)
+    by_target = column_products(comp, before, after, scale_kernels, col_taper[0], col_inverse)
+    regrouped = lax.all_to_all(by_target, "strip", split_axis=0, concat_axis=0, tiled=True)
+    all_rows = row_taper[0].reshape(n_strip, rows, sub_rows, contrib_side)
     finished = jnp.einsum(
-        "rai,crj->acij", all_rows, regrouped[:, :, 0, :], preferred_element_type=jnp.float32
+        "xrai,xcrj->acij", all_rows, regrouped, preferred_element_type=jnp.float32
     ).astype(jnp.bfloat16)
     outgoing = jnp.take(finished, row_inverse, axis=0)
     mine = lax.all_to_all(outgoing, "facet", split_axis=0, concat_axis=0, tiled=True)
@@ -145,9 +273,7 @@
         tiled=True,
     ).astype(outgoing_vis.dtype)
     placed = arrived.reshape(devices * capacity, corr, visibility_block)
-    gain_p = jnp.take(gains, antenna_pair_index[:, 0, :], axis=1)
-    gain_q = jnp.take(gains, antenna_pair_index[:, 1, :], axis=1)
-    product = jnp.transpose(gain_p * gain_q, (1, 0, 2))
+    product = gain_products(gains, antenna_pair_index)
     residual = observed - product * placed
     return (subgrid[None], residual)
 

time: 666 us -> 110 us (0.17)
  other arithmetic: 470 us -> 15.5 us
  local copies, waits for them, and re-layouts: 136 us -> 12.1 us
  Pallas kernels: 0 us -> 23.3 us
    reduce_sum x1 -> x0, other arithmetic: 325 us -> none  [smooth_rows_cols(): return jnp.sum(total, axis=1).astype(jnp.bfloat16)]
    add x1 -> x0, other arithmetic: 136 us -> none  [smooth_rows_cols(): along_rows + kernels[:, tap][None, :, None, None] * padded[:, :, tap:tap...]
    gather x5 -> x0, local copies, waits for them, and re-layouts: 120 us -> none  [the longest x2 59.6 us: on_device(): gain_q = jnp.take(gains, antenna_pair_index[:, 1, :], axis=1)]
    pallas_call x0 -> x2, Pallas kernels: none -> 23.3 us  [the longest x1 20.1 us: column_products(): pl.pallas_call(smooth_kernel, grid_spec=pltpu.PrefetchScalarGridSpec(num_...]
  transfers between devices with their start and end apart: 5 -> 5, of which waited for: 2 -> 3; matrix products, arithmetic and copies ran while one was open for 20% -> 14% of each run, Pallas kernels for 0% -> 3%
where the time goes in v1:
time: 110 us
  Pallas kernels  23.3 us (21%)
  waiting for transfers between devices  21.9 us (20%)
  starting transfers between devices  19.9 us (18%)
  matrix products  15.8 us (14%)
  other arithmetic  15.5 us (14%)
  local copies, waits for them, and re-layouts  12.1 us (11%)
    pallas_call x1, Pallas kernels, column_products(): pl.pallas_call(smooth_kernel, grid_spec=pltpu.PrefetchScalarGridSpec(num_...  20.1 us
    all_to_all x1, waiting for transfers between devices, on_device(): lax.all_to_all(by_target, 'strip', split_axis=0, concat_axis=0, tiled=True)  12.5 us
    dot_general x2, matrix products, predict_group(): jnp.einsum('kvx,cxy->kcvy', row_weights, subgrid, preferred_element_type=...  11.9 us
    all_to_all x1, starting transfers between devices, on_device(): lax.all_to_all(by_target, 'strip', split_axis=0, concat_axis=0, tiled=True)  7.18 us
    all_to_all x1, waiting for transfers between devices, on_device(): lax.all_to_all(outgoing, 'facet', split_axis=0, concat_axis=0, tiled=True)  6.49 us
    select_n x2, other arithmetic, window_weights(): return jnp.where(inside[:, None, :], jnp.exp(-0.5 * delta * delta), 0.0)  5.32 us
    all_to_all x1, starting transfers between devices, on_device(): lax.all_to_all(outgoing, 'facet', split_axis=0, concat_axis=0, tiled=True)  4.86 us
    all_to_all x1, starting transfers between devices, on_device(): lax.all_to_all(outgoing_vis.astype(jnp.bfloat16), ('facet', 'strip'), spl...  4.12 us
  transfers between devices with their start and end apart: 5, of which 3 were waited for; matrix products, arithmetic and copies ran while one was open for 14% of the time, Pallas kernels for 3%

profile of v1, /device:TPU:0, one launch (start us, length us, event | category | flops | bytes accessed | tf_op | source)
XLA Modules:
  0.0 109.7 jit_solution(278884625985058232)
XLA Ops:
  0.6 0.0 copy-start
  0.6 1.4 %fusion.124 = (bf16[2,4,16,2048]{3,2,1,0:T(8,128)(2,1)S(1)}, bf16[2,4,16,2048]{3,2,1,0:T(8,128)(2,1)S(1)}) fusion(bf16[2,4,256,2048]{3,2,1,0:T(8,128)(2,1)} %bitcast.115), kind=kLoop, calls=%fused_computation.199 | loop fusion | bytes 2097152 | tf_op jit(solution)/shard_map/slice | solution.py:23
  2.0 2.4 %collective-permute-start = (bf16[2,4,16,2048]{3,2,1,0:T(8,128)(2,1)S(1)}, bf16[2,4,16,2048]{3,2,1,0:T(8,128)(2,1)S(1)}, u32[]{:S(2)}, u32[]{:S(2)}) collective-permute-start(bf16[2,4,16,2048]{3,2,1,0:T(8,128)(2,1)S(1)} %get-tuple-element.171), channel_id=1, source_target_pairs={{0,1},{1,2},{2,3},{3,4},{4,5},{5,6},{6,7},{8,9},{9,10},{10,11},{11... | collective-permute-start | bytes 1572872 | tf_op jit(solution)/shard_map/ppermute | solution.py:24
  4.5 1.3 %collective-permute-start.1 = (bf16[2,4,16,2048]{3,2,1,0:T(8,128)(2,1)S(1)}, bf16[2,4,16,2048]{3,2,1,0:T(8,128)(2,1)S(1)}, u32[]{:S(2)}, u32[]{:S(2)}) collective-permute-start(bf16[2,4,16,2048]{3,2,1,0:T(8,128)(2,1)S(1)} %get-tuple-element.170), channel_id=1, source_target_pairs={{1,0},{2,1},{3,2},{4,3},{5,4},{6,5},{7,6},{9,8},{10,9},{11,10},{12... | collective-permute-start | bytes 1572872 | tf_op jit(solution)/shard_map/ppermute | solution.py:24
  5.8 1.9 %slice_reduce_fusion.32 = (bf16[4]{0:T(256)(128)(2,1)S(1)}, bf16[4]{0:T(256)(128)(2,1)S(1)}, bf16[4]{0:T(256)(128)(2,1)S(1)}, bf16[4]{0:T(256)(128)(2,1)S(1)}, b...) fusion(f32[4,33]{1,0:T(4,128)} %param.16), kind=kLoop, calls=%fused_computation.186 | loop fusion | bytes 456 | tf_op jit(solution)/shard_map/slice | solution.py:38
  7.6 1.6 %slice_reduce_fusion.31 = (bf16[4]{0:T(256)(128)(2,1)S(1)}, bf16[4]{0:T(256)(128)(2,1)S(1)}, bf16[4]{0:T(256)(128)(2,1)S(1)}, bf16[4]{0:T(256)(128)(2,1)S(1)}, b...) fusion(f32[4,33]{1,0:T(4,128)} %param.16), kind=kLoop, calls=%fused_computation.185 | loop fusion | bytes 336 | tf_op jit(solution)/shard_map/slice | solution.py:38
  10.5 1.2 %select_convert_fusion.1 = bf16[4,160,128]{2,1,0:T(8,128)(2,1)S(1)} fusion(bf16[4]{0:T(256)(128)(2,1)S(1)} %get-tuple-element.150, bf16[4]{0:T(256)(128)(2,1)S(1)} %get-tuple-element.151, bf16[4]{0:T(256)(128)(2,1)S(1)} %get-tuple-element.120, bf16[4]{0:T(256)(128)(2,1)S(1)} %get-tuple-element.121, bf16[4]{0:T(256)(128)(2,1)S(1)} %get-tuple-element.122, ...), kind=kLoop, calls=%fused_computation.61 | loop fusion | flops 2703360 | bytes 839944 | tf_op jit(solution)/shard_map/convert_element_type | solution.py:41
  11.7 1.0 fusion.41.cols_ref
  12.7 0.7 and_select_fusion
  13.4 0.6 select_reduce_fusion.order_ref
  14.0 2.5 %select_convert_fusion.rows_ref = bf16[4,128,160]{2,1,0:T(8,128)(2,1)} fusion(bf16[4]{0:T(256)(128)(2,1)S(1)} %get-tuple-element.150, bf16[4]{0:T(256)(128)(2,1)S(1)} %get-tuple-element.151, bf16[4]{0:T(256)(128)(2,1)S(1)} %get-tuple-element.120, bf16[4]{0:T(256)(128)(2,1)S(1)} %get-tuple-element.121, bf16[4]{0:T(256)(128)(2,1)S(1)} %get-tuple-element.122, ...), kind=kLoop, calls=%fused_computation.60 | loop fusion | flops 2703360 | bytes 839944 | tf_op jit(solution)/shard_map/convert_element_type | solution.py:41
  16.5 0.0 collective-permute-done.before_ref
  16.5 0.0 copy-start.3
  16.5 0.0 collective-permute-done.1.after_ref
  16.6 0.0 copy-start.4
  16.6 0.8 copy-done.3
  17.3 0.2 copy-done.4
  17.5 0.0 copy-start.2
  17.5 0.0 copy-start.1
  17.5 20.1 %column_products.1 = bf16[8,2,256,128]{3,2,1,0:T(8,128)(2,1)} custom-call(s32[8]{0:T(128)} %select_reduce_fusion.order_ref, bf16[2,4,256,2048]{3,2,1,0:T(8,128)(2,1)} %bitcast.116, bf16[2,4,16,2048]{3,2,1,0:T(8,128)(2,1)} %copy-done.3, bf16[2,4,16,2048]{3,2,1,0:T(8,128)(2,1)} %copy-done.4, bf16[4,128,160]{2,1,0:T(8,128)(2,1)} %select_convert_fusion.rows_ref, ...), custom_call_target="tpu_custom_call" | custom-call | tf_op jit(solution)/shard_map/column_products/pallas_call | solution.py:114
  37.6 0.0 copy-start.7
  37.6 0.0 copy-start.9
  37.6 7.2 %all-to-all-start = ((bf16[8,2,256,128]{3,2,1,0:T(8,128)(2,1)}), bf16[8,2,256,128]{3,2,1,0:T(8,128)(2,1)}, u32[]{:S(2)}, u32[]{:S(2)}) async-start(bf16[8,2,256,128]{3,2,1,0:T(8,128)(2,1)} %column_products.1), calls=%async_computation | async-start | bytes 2097152 | tf_op jit(solution)/shard_map/all_to_all | solution.py:222
  44.8 0.0 copy-done.2
  44.8 0.0 copy-start.8
  44.8 0.0 copy-start.5
  44.8 2.1 %reshape_squeeze.3 = bf16[8,256,4,128]{3,2,1,0:T(4,128)(2,1)} reshape(bf16[1,2048,512]{2,1,0:T(8,128)(2,1)S(1)} %copy-done.2) | data formatting | bytes 4194304 | tf_op jit(solution)/shard_map/reshape;squeeze | solution.py:223
  46.9 0.0 copy-done.1
  46.9 0.6 gather_fusion
  47.6 0.1 select_reduce_fusion.1
  47.7 12.5 %all-to-all-done = bf16[8,2,256,128]{3,2,1,0:T(8,128)(2,1)} async-done(((bf16[8,2,256,128]{3,2,1,0:T(8,128)(2,1)}), bf16[8,2,256,128]{3,2,1,0:T(8,128)(2,1)}, u32[]{:S(2)}, u32[]{:S(2)}) %all-to-all-start) | async-done | bytes 1048608 | tf_op jit(solution)/shard_map/all_to_all | solution.py:222
  60.3 2.7 %fusion.38 = bf16[4,2,128,128]{2,3,1,0:T(8,128)(2,1)S(1)} fusion(bf16[8,256,4,128,1]{3,2,1,0,4:T(4,128)(2,1)} %bitcast.121, bf16[8,2,256,128]{3,2,1,0:T(8,128)(2,1)} %all-to-all-done), kind=kOutput, calls=%fused_computation.54 | convolution fusion | flops 537001984 | bytes 3407872 | tf_op jit(solution)/shard_map/xrai,xcrj->acij/dot_general | solution.py:224
  62.9 0.2 copy.52
  63.1 0.6 gather_fusion.1
  63.7 0.8 broadcast_select_fusion
  64.5 4.9 %all-to-all-start.1 = ((bf16[4,2,128,128]{3,2,1,0:T(8,128)(2,1)}), bf16[4,2,128,128]{3,2,1,0:T(8,128)(2,1)S(1)}, u32[]{:S(2)}, u32[]{:S(2)}) async-start(bf16[4,2,128,128]{3,2,1,0:T(8,128)(2,1)} %broadcast_select_fusion), calls=%async_computation.1 | async-start | bytes 524288 | tf_op jit(solution)/shard_map/all_to_all | solution.py:228
  69.4 0.0 copy-done.7
  69.4 0.1 reshape.567
  69.5 0.0 copy-done.9
  69.5 0.2 convert_reduce_fusion
  69.7 6.5 %all-to-all-done.1 = bf16[4,2,128,128]{3,2,1,0:T(8,128)(2,1)S(1)} async-done(((bf16[4,2,128,128]{3,2,1,0:T(8,128)(2,1)}), bf16[4,2,128,128]{3,2,1,0:T(8,128)(2,1)S(1)}, u32[]{:S(2)}, u32[]{:S(2)}) %all-to-all-start.1) | async-done | bytes 262176 | tf_op jit(solution)/shard_map/all_to_all | solution.py:228
  76.2 0.0 copy-done
  76.2 0.0 copy-done.8
  76.2 1.0 bitcast_convert_fusion
  77.1 0.5 copy.58
  77.7 0.0 copy-done.5
  77.7 0.0 copy-start.6
  77.7 17.9 %while.13 = (s32[]{:T(128)}, f32[2,32,2,128]{3,2,1,0:T(2,128)S(1)}, s32[2,32,2]{1,0,2:T(2,128)S(1)}, f32[2,32,2,128]{3,2,1,0:T(2,128)S(1)}, bf16[2,512,512]{2,1,0:T(8,128)(2,1)S(1)}, /*index=5*/s32[]{:T(128)}) while((s32[]{:T(128)}, f32[2,32,2,128]{3,2,1,0:T(2,128)S(1)}, s32[2,32,2]{1,0,2:T(2,128)S(1)}, f32[2,32,2,128]{3,2,1,0:T(2,128)S(1)}, ...), condition=%wide.region_5.6_spmd, body=%wide.region_3.5_spmd.sunk | while | flops 4326612992 | bytes 18482768 | solution.py:252
  77.8 0.1 fusion.132
  77.8 0.1 fusion.133
  78.0 2.7 %fusion.134 = f32[32,128,512]{2,1,0:T(8,128)S(1)} fusion(f32[32,128]{1,0:T(8,128)S(1)} %get-tuple-element.275, f32[32,512]{1,0:T(8,128)S(1)} %get-tuple-element.278, pred[32,512]{1,0:T(8,128)(4,1)S(1)} %get-tuple-element.279), kind=kLoop, calls=%fused_computation.13.clone.1 | loop fusion | flops 10485760 | bytes 8486912 | tf_op jit(solution)/shard_map/while/body/eval_jaxpr/jit(_where)/select_n | solution.py:179
  80.7 6.0 %multiply_reduce_fusion.2 = f32[32,128,2]{1,2,0:T(2,128)S(1)} fusion(f32[32,128,512]{2,1,0:T(8,128)S(1)} %fusion.134, f32[32,128]{1,0:T(8,128)S(1)} %get-tuple-element.280, f32[32,512]{1,0:T(8,128)S(1)} %get-tuple-element.281, pred[32,512]{1,0:T(8,128)(4,1)S(1)} %get-tuple-element.282, bf16[2,512,512]{2,1,0:T(8,128)(2,1)S(1)} %get-tuple-element.299), kind=kOutput, calls=%fused_computation.2.clone.1 | convolution fusion | flops 4315930624 | bytes 9568256 | tf_op jit(solution)/shard_map/while/body/eval_jaxpr/kvx,cxy->kcvy/dot_general | solution.py:245
  86.7 0.1 fusion.132
  86.8 0.1 fusion.133
  86.9 2.7 %fusion.134 = f32[32,128,512]{2,1,0:T(8,128)S(1)} fusion(f32[32,128]{1,0:T(8,128)S(1)} %get-tuple-element.275, f32[32,512]{1,0:T(8,128)S(1)} %get-tuple-element.278, pred[32,512]{1,0:T(8,128)(4,1)S(1)} %get-tuple-element.279), kind=kLoop, calls=%fused_computation.13.clone.1 | loop fusion | flops 10485760 | bytes 8486912 | tf_op jit(solution)/shard_map/while/body/eval_jaxpr/jit(_where)/select_n | solution.py:179
  89.6 6.0 %multiply_reduce_fusion.2 = f32[32,128,2]{1,2,0:T(2,128)S(1)} fusion(f32[32,128,512]{2,1,0:T(8,128)S(1)} %fusion.134, f32[32,128]{1,0:T(8,128)S(1)} %get-tuple-element.280, f32[32,512]{1,0:T(8,128)S(1)} %get-tuple-element.281, pred[32,512]{1,0:T(8,128)(4,1)S(1)} %get-tuple-element.282, bf16[2,512,512]{2,1,0:T(8,128)(2,1)S(1)} %get-tuple-element.299), kind=kOutput, calls=%fused_computation.2.clone.1 | convolution fusion | flops 4315930624 | bytes 9568256 | tf_op jit(solution)/shard_map/while/body/eval_jaxpr/kvx,cxy->kcvy/dot_general | solution.py:245
  95.6 0.3 convolution_convert_fusion.1
  95.9 0.7 copy.60
  96.5 4.1 %all-to-all-start.2 = ((bf16[32,4,2,128]{3,2,1,0:T(2,128)(2,1)}), bf16[32,4,2,128]{3,2,1,0:T(2,128)(2,1)S(1)}, u32[]{:S(2)}, u32[]{:S(2)}) async-start(bf16[32,4,2,128]{3,2,1,0:T(2,128)(2,1)} %copy.60), calls=%async_computation.2 | async-start | bytes 131072 | tf_op jit(solution)/shard_map/all_to_all | solution.py:268
  100.7 3.3 %gain_products.1 = f32[128,2,128]{2,1,0:T(2,128)} custom-call(f32[2,512]{1,0:T(2,128)} %gains_ref.1, s32[128,2,128]{2,1,0:T(2,128)} %index_ref.1), custom_call_target="tpu_custom_call" | custom-call | tf_op jit(solution)/shard_map/gain_products/pallas_call | solution.py:161
  103.9 1.3 %copy.61 = bf16[1,2,512,512]{3,2,1,0:T(8,128)(2,1)} copy(bf16[1,2,512,512]{2,3,1,0:T(8,128)(2,1)S(1)} %bitcast.119) | data formatting | bytes 2097152
  105.2 2.8 %all-to-all-done.2 = bf16[32,4,2,128]{3,2,1,0:T(2,128)(2,1)S(1)} async-done(((bf16[32,4,2,128]{3,2,1,0:T(2,128)(2,1)}), bf16[32,4,2,128]{3,2,1,0:T(2,128)(2,1)S(1)}, u32[]{:S(2)}, u32[]{:S(2)}) %all-to-all-start.2) | async-done | bytes 65568 | tf_op jit(solution)/shard_map/all_to_all | solution.py:268
  108.1 0.0 copy-done.6
  108.1 1.7 %fusion.48 = f32[128,2,128]{2,1,0:T(2,128)} fusion(f32[128,2,128]{2,1,0:T(2,128)S(1)} %copy-done.6, f32[128,2,128]{2,1,0:T(2,128)} %gain_products.1, bf16[32,4,2,128]{3,2,1,0:T(2,128)(2,1)S(1)} %all-to-all-done.2), kind=kLoop, calls=%fused_computation.65 | loop fusion | flops 98304 | bytes 458752 | tf_op jit(solution)/shard_map/sub | solution.py:277
  (55 shorter events, 1.1 us)
Async XLA Ops:
  0.6 75.5 %copy-start = (bf16[4,512,128]{2,1,0:T(8,128)(2,1)S(1)}, bf16[4,512,128]{2,1,0:T(8,128)(2,1)}, u32[]{:S(2)}) copy-start(bf16[4,512,128]{2,1,0:T(8,128)(2,1)} %param.19) | copy-start | bytes 1572868
  2.0 14.5 %collective-permute-start = (bf16[2,4,16,2048]{3,2,1,0:T(8,128)(2,1)S(1)}, bf16[2,4,16,2048]{3,2,1,0:T(8,128)(2,1)S(1)}, u32[]{:S(2)}, u32[]{:S(2)}) collective-permute-start(bf16[2,4,16,2048]{3,2,1,0:T(8,128)(2,1)S(1)} %get-tuple-element.171), channel_id=1, source_target_pairs={{0,1},{1,2},{2,3},{3,4},{4,5},{5,6},{6,7},{8,9},{9,10},{10,11},{11... | collective-permute-start | bytes 1572872 | tf_op jit(solution)/shard_map/ppermute | solution.py:24
  4.5 12.1 %collective-permute-start.1 = (bf16[2,4,16,2048]{3,2,1,0:T(8,128)(2,1)S(1)}, bf16[2,4,16,2048]{3,2,1,0:T(8,128)(2,1)S(1)}, u32[]{:S(2)}, u32[]{:S(2)}) collective-permute-start(bf16[2,4,16,2048]{3,2,1,0:T(8,128)(2,1)S(1)} %get-tuple-element.170), channel_id=1, source_target_pairs={{1,0},{2,1},{3,2},{4,3},{5,4},{6,5},{7,6},{9,8},{10,9},{11,10},{12... | collective-permute-start | bytes 1572872 | tf_op jit(solution)/shard_map/ppermute | solution.py:24
  16.5 0.8 copy-start.3
  16.6 1.0 copy-start.4
  17.5 27.3 %copy-start.2 = (bf16[1,2048,512]{2,1,0:T(8,128)(2,1)S(1)}, bf16[1,2048,512]{2,1,0:T(8,128)(2,1)}, u32[]{:S(2)}) copy-start(bf16[1,2048,512]{2,1,0:T(8,128)(2,1)} %param.17) | copy-start | bytes 6291460
  17.5 29.4 %copy-start.1 = (s32[32]{0:T(128)S(1)}, s32[32]{0:T(128)}, u32[]{:S(2)}) copy-start(s32[32]{0:T(128)} %param.21) | copy-start | bytes 388
  37.6 31.8 %copy-start.7 = (s32[64,2]{0,1:T(2,128)S(1)}, s32[64,2]{0,1:T(2,128)}, u32[]{:S(2)}) copy-start(s32[64,2]{0,1:T(2,128)} %param.22) | copy-start | bytes 1540
  37.6 31.9 %copy-start.9 = (s32[64,1]{0,1:T(1,128)S(1)}, s32[64,1]{0,1:T(1,128)}, u32[]{:S(2)}) copy-start(s32[64,1]{0,1:T(1,128)} %param.24) | copy-start | bytes 772
  37.6 22.7 %all-to-all-start = ((bf16[8,2,256,128]{3,2,1,0:T(8,128)(2,1)}), bf16[8,2,256,128]{3,2,1,0:T(8,128)(2,1)}, u32[]{:S(2)}, u32[]{:S(2)}) async-start(bf16[8,2,256,128]{3,2,1,0:T(8,128)(2,1)} %column_products.1), calls=%async_computation | async-start | bytes 2097152 | tf_op jit(solution)/shard_map/all_to_all | solution.py:222
  44.8 31.4 %copy-start.8 = (bf16[4,512,128]{2,1,0:T(8,128)(2,1)S(1)}, bf16[4,512,128]{2,1,0:T(8,128)(2,1)}, u32[]{:S(2)}) copy-start(bf16[4,512,128]{2,1,0:T(8,128)(2,1)} %param.20) | copy-start | bytes 1572868
  44.8 32.9 %copy-start.5 = (f32[64,2,128]{2,1,0:T(2,128)S(1)}, f32[64,2,128]{2,1,0:T(2,128)}, u32[]{:S(2)}) copy-start(f32[64,2,128]{2,1,0:T(2,128)} %param.23) | copy-start | bytes 196612
  64.5 11.6 %all-to-all-start.1 = ((bf16[4,2,128,128]{3,2,1,0:T(8,128)(2,1)}), bf16[4,2,128,128]{3,2,1,0:T(8,128)(2,1)S(1)}, u32[]{:S(2)}, u32[]{:S(2)}) async-start(bf16[4,2,128,128]{3,2,1,0:T(8,128)(2,1)} %broadcast_select_fusion), calls=%async_computation.1 | async-start | bytes 524288 | tf_op jit(solution)/shard_map/all_to_all | solution.py:228
  77.7 30.4 %copy-start.6 = (f32[128,2,128]{2,1,0:T(2,128)S(1)}, f32[128,2,128]{2,1,0:T(2,128)}, u32[]{:S(2)}) copy-start(f32[128,2,128]{2,1,0:T(2,128)} %param.25) | copy-start | bytes 393220
  96.5 11.5 %all-to-all-start.2 = ((bf16[32,4,2,128]{3,2,1,0:T(2,128)(2,1)}), bf16[32,4,2,128]{3,2,1,0:T(2,128)(2,1)S(1)}, u32[]{:S(2)}, u32[]{:S(2)}) async-start(bf16[32,4,2,128]{3,2,1,0:T(2,128)(2,1)} %copy.60), calls=%async_computation.2 | async-start | bytes 131072 | tf_op jit(solution)/shard_map/all_to_all | solution.py:268

commit v2 on v1

--- a/solution.py
+++ b/solution.py
@@ -171,12 +171,81 @@
     )(gains, index)
 
 
-def window_weights(corner, offset, grid_side, tile_side):
-    places = jnp.arange(grid_side, dtype=jnp.int32)
-    relative = places[None, :] - corner[:, None]
-    inside = (relative >= 0) & (relative < tile_side)
-    delta = (relative.astype(jnp.float32)[:, None, :] - offset[:, :, None]) / KERNEL_WIDTH
-    return jnp.where(inside[:, None, :], jnp.exp(-0.5 * delta * delta), 0.0)
+ALIGN = 16
+
+
+def degrid_kernel(corner_ref, target_ref, mine_ref, cols_ref, rows_ref, offset_ref, subgrid_ref, out_ref, turned_ref):
+    facets, corr = mine_ref.shape[0], mine_ref.shape[1]
+    side = cols_ref.shape[1]
+    blocks, vis = offset_ref.shape[0], offset_ref.shape[2]
+    tall, wide = TILE + ALIGN, 2 * LANES
+    row_mats = jnp.concatenate([rows_ref[f] for f in range(facets)], axis=1)
+    across = (((1,), (1,)), ((), ()))
+    for c in range(corr):
+        spread = jnp.concatenate(
+            [
+                lax.dot_general(
+                    cols_ref[f], mine_ref[f, c], across, preferred_element_type=jnp.float32
+                ).astype(jnp.bfloat16)
+                for f in range(facets)
+            ],
+            axis=1,
+        )
+        subgrid_ref[c] = lax.dot_general(
+            row_mats, spread, across, preferred_element_type=jnp.float32
+        ).astype(jnp.bfloat16)
+        turned_ref[c] = lax.dot_general(
+            spread, row_mats, across, preferred_element_type=jnp.float32
+        ).astype(jnp.bfloat16)
+    out_ref[...] = jnp.zeros_like(out_ref)
+    row_places = lax.broadcasted_iota(jnp.int32, (wide, vis), 0)
+    col_places = lax.broadcasted_iota(jnp.int32, (tall, vis), 0)
+    factor = -0.5 / (KERNEL_WIDTH * KERNEL_WIDTH)
+
+    def weights(places, offset):
+        delta = places.astype(jnp.float32) - offset
+        inside = (places >= 0) & (places < TILE)
+        return jnp.where(inside, jnp.exp(factor * (delta * delta)), 0.0)
+
+    def one_block(k, carry):
+        r, q = corner_ref[k, 0], corner_ref[k, 1]
+        r0 = pl.multiple_of(jnp.minimum(r // LANES * LANES, side - wide), LANES)
+        q0 = pl.multiple_of(jnp.minimum(q // ALIGN * ALIGN, side - tall), ALIGN)
+        offsets = offset_ref[k]
+        row_weights = weights(row_places - (r - r0), offsets[0:1]).astype(jnp.bfloat16)
+        col_weights = weights(col_places - (q - q0), offsets[1:2])
+        tile = jnp.concatenate(
+            [turned_ref[c, pl.ds(q0, tall), pl.ds(r0, wide)] for c in range(corr)], axis=0
+        )
+        along = jnp.dot(tile, row_weights, preferred_element_type=jnp.float32)
+        values = [
+            jnp.sum(along[c * tall : (c + 1) * tall] * col_weights, axis=0, keepdims=True)
+            for c in range(corr)
+        ]
+        out_ref[target_ref[k]] = jnp.concatenate(values, axis=0).astype(out_ref.dtype)
+        return carry
+
+    lax.fori_loop(0, blocks, one_block, 0, unroll=4)
+
+
+def formed_and_predicted(mine, finish_cols, finish_rows, corners, offsets, target, slots):
+    corr = mine.shape[1]
+    side = finish_cols.shape[1]
+    vis = offsets.shape[2]
+    whole = pl.BlockSpec(memory_space=pltpu.VMEM)
+    scalars = pl.BlockSpec(memory_space=pltpu.SMEM)
+    return pl.pallas_call(
+        degrid_kernel,
+        in_specs=[scalars, scalars, whole, whole, whole, whole],
+        out_specs=[whole, whole],
+        out_shape=[
+            jax.ShapeDtypeStruct((corr, side, side), jnp.bfloat16),
+            jax.ShapeDtypeStruct((slots, corr, vis), jnp.bfloat16),
+        ],
+        scratch_shapes=[pltpu.VMEM((corr, side, side), jnp.bfloat16)],
+        compiler_params=pltpu.CompilerParams(vmem_limit_bytes=32 * 1024 * 1024),
+        name="formed_and_predicted",
+    )(corners, target, mine, finish_cols, finish_rows, offsets)
 
 
 def inverse_of(perm):
@@ -208,11 +277,9 @@
     rows = comp.shape[2]
     facet_side = comp.shape[3]
     contrib_side = finish_cols.shape[2]
-    grid_side = finish_cols.shape[1]
     sub_rows = row_taper.shape[2] // contrib_side
     sub_cols = col_taper.shape[2] // contrib_side
     width = (scale_kernels.shape[1] - 1) // 2
-    tile_side = TILE
     before, after = halo_rows(comp, "strip", 2, width)
     col_perm = subgrid_owner[:sub_cols] % n_strip
     row_perm = subgrid_owner[jnp.arange(sub_rows, dtype=jnp.int32) * sub_cols] // n_strip
@@ -226,32 +293,8 @@
     ).astype(jnp.bfloat16)
     outgoing = jnp.take(finished, row_inverse, axis=0)
     mine = lax.all_to_all(outgoing, "facet", split_axis=0, concat_axis=0, tiled=True)
-    spread = jnp.einsum(
-        "fcij,fsj->fcis", mine, finish_cols, preferred_element_type=jnp.float32
-    ).astype(jnp.bfloat16)
-    subgrid = jnp.einsum(
-        "fri,fcis->crs", finish_rows, spread, preferred_element_type=jnp.float32
-    ).astype(jnp.bfloat16)
     blocks = block_owner.shape[0]
-    group = min(blocks, 32)
     visibility_block = observed.shape[2]
-
-    def predict_group(pieces):
-        cells, offsets = pieces
-        row_weights = window_weights(cells[:, 0], offsets[:, 0, :], grid_side, tile_side).astype(
-            jnp.bfloat16
-        )
-        col_weights = window_weights(cells[:, 1], offsets[:, 1, :], grid_side, tile_side)
-        along = jnp.einsum(
-            "kvx,cxy->kcvy", row_weights, subgrid, preferred_element_type=jnp.float32
-        )
-        return jnp.sum(along * col_weights[:, None, :, :], axis=3)
-
-    grouped_cells = block_cell.reshape(blocks // group, group, 2)
-    grouped_offsets = vis_offset.reshape(blocks // group, group, 2, visibility_block)
-    predicted = lax.map(predict_group, (grouped_cells, grouped_offsets)).reshape(
-        blocks, corr * visibility_block
-    )
     dest = block_owner[:, 0]
     same = dest[:, None] == dest[None, :]
     order = jnp.arange(blocks, dtype=jnp.int32)
@@ -259,19 +302,13 @@
     rank = jnp.sum((same & earlier).astype(jnp.int32), axis=1)
     capacity = observed.shape[0] // devices
     target = dest * capacity + rank
-    slots = jnp.arange(devices * capacity, dtype=jnp.int32)
-    placing = (slots[:, None] == target[None, :]).astype(jnp.float32)
-    outgoing_vis = jnp.dot(
-        placing, predicted, precision=lax.Precision.HIGHEST, preferred_element_type=jnp.float32
+    subgrid, outgoing_vis = formed_and_predicted(
+        mine, finish_cols, finish_rows, block_cell, vis_offset, target, devices * capacity
     )
     outgoing_vis = outgoing_vis.reshape(devices, capacity, corr, visibility_block)
     arrived = lax.all_to_all(
-        outgoing_vis.astype(jnp.bfloat16),
-        ("facet", "strip"),
-        split_axis=0,
-        concat_axis=0,
-        tiled=True,
-    ).astype(outgoing_vis.dtype)
+        outgoing_vis, ("facet", "strip"), split_axis=0, concat_axis=0, tiled=True
+    ).astype(jnp.float32)
     placed = arrived.reshape(devices * capacity, corr, visibility_block)
     product = gain_products(gains, antenna_pair_index)
     residual = observed - product * placed

time: 110 us -> 97.8 us (0.89)
  matrix products: 15.8 us -> 2.35 us
  Pallas kernels: 23.3 us -> 32.7 us
  other arithmetic: 15.5 us -> 9.16 us
  local copies, waits for them, and re-layouts: 12.1 us -> 6.85 us
  starting transfers between devices: 19.9 us -> 22.1 us
  waiting for transfers between devices: 21.9 us -> 23.1 us
    dot_general x4 -> x0, matrix products: 13.2 us -> none  [the longest x2 11.9 us: predict_group(): jnp.einsum('kvx,cxy->kcvy', row_weights, subgrid, preferred_element_type=...]
    pallas_call x0 -> x1, Pallas kernels: none -> 9.51 us  [formed_and_predicted(): pl.pallas_call(degrid_kernel, in_specs=[scalars, scalars, whole, whole, w...]
    select_n x2 -> x0, other arithmetic: 5.32 us -> none  [window_weights(): return jnp.where(inside[:, None, :], jnp.exp(-0.5 * delta * delta), 0.0)]
    slice x2, local copies, waits for them, and re-layouts: 3.5 us -> 0.91 us  [band_matrices(): tap = kernels[:, t][:, None, None]]
    all_to_all x1, starting transfers between devices: 7.18 us -> 9.4 us  [on_device(): lax.all_to_all(by_target, 'strip', split_axis=0, concat_axis=0, tiled=True)]
    all_to_all x1, waiting for transfers between devices: 2.83 us -> 4.15 us  [on_device(): lax.all_to_all(outgoing_vis, ('facet', 'strip'), split_axis=0, concat_axi...]
    unnamed x21 -> x23, local copies, waits for them, and re-layouts: 2.33 us -> 1.12 us
  transfers between devices with their start and end apart: 5 -> 5, of which waited for: 3 -> 3; matrix products, arithmetic and copies ran while one was open for 14% -> 11% of each run, Pallas kernels for 3% -> 3%
where the time goes in v2:
time: 97.8 us; the launch traced here: 97.4 us
  Pallas kernels  32.7 us (33%)
  waiting for transfers between devices  23.1 us (24%)
  starting transfers between devices  22.1 us (23%)
  other arithmetic  9.16 us (9%)
  local copies, waits for them, and re-layouts  6.85 us (7%)
  matrix products  2.35 us (2%)
  between operations  1.07 us (1%)
    pallas_call x1, Pallas kernels, column_products(): pl.pallas_call(smooth_kernel, grid_spec=pltpu.PrefetchScalarGridSpec(num_...  19.9 us
    all_to_all x1, waiting for transfers between devices, on_device(): lax.all_to_all(by_target, 'strip', split_axis=0, concat_axis=0, tiled=True)  12.5 us
    pallas_call x1, Pallas kernels, formed_and_predicted(): pl.pallas_call(degrid_kernel, in_specs=[scalars, scalars, whole, whole, w...  9.51 us
    all_to_all x1, starting transfers between devices, on_device(): lax.all_to_all(by_target, 'strip', split_axis=0, concat_axis=0, tiled=True)  9.4 us
    all_to_all x1, waiting for transfers between devices, on_device(): lax.all_to_all(outgoing, 'facet', split_axis=0, concat_axis=0, tiled=True)  6.49 us
    all_to_all x1, starting transfers between devices, on_device(): lax.all_to_all(outgoing, 'facet', split_axis=0, concat_axis=0, tiled=True)  4.86 us
    all_to_all x1, starting transfers between devices, on_device(): lax.all_to_all(outgoing_vis, ('facet', 'strip'), split_axis=0, concat_axi...  4.17 us
    all_to_all x1, waiting for transfers between devices, on_device(): lax.all_to_all(outgoing_vis, ('facet', 'strip'), split_axis=0, concat_axi...  4.15 us
  transfers between devices with their start and end apart: 5, of which 3 were waited for; matrix products, arithmetic and copies ran while one was open for 11% of the time, Pallas kernels for 3%

profile of v2, /device:TPU:0, one launch (start us, length us, event | category | flops | bytes accessed | tf_op | source)
XLA Modules:
  0.0 97.4 jit_solution(18230964292889009702)
XLA Ops:
  0.6 0.0 copy-start.4
  0.6 1.3 %fusion.87 = (bf16[2,4,16,2048]{3,2,1,0:T(8,128)(2,1)S(1)}, bf16[2,4,16,2048]{3,2,1,0:T(8,128)(2,1)S(1)}) fusion(bf16[2,4,256,2048]{3,2,1,0:T(8,128)(2,1)} %bitcast.37), kind=kLoop, calls=%fused_computation.144 | loop fusion | bytes 2097152 | tf_op jit(solution)/shard_map/slice | solution.py:23
  2.0 0.0 copy-start.3
  2.0 2.4 %collective-permute-start = (bf16[2,4,16,2048]{3,2,1,0:T(8,128)(2,1)S(1)}, bf16[2,4,16,2048]{3,2,1,0:T(8,128)(2,1)S(1)}, u32[]{:S(2)}, u32[]{:S(2)}) collective-permute-start(bf16[2,4,16,2048]{3,2,1,0:T(8,128)(2,1)S(1)} %get-tuple-element.40), channel_id=1, source_target_pairs={{0,1},{1,2},{2,3},{3,4},{4,5},{5,6},{6,7},{8,9},{9,10},{10,11},{11... | collective-permute-start | bytes 1572872 | tf_op jit(solution)/shard_map/ppermute | solution.py:24
  4.4 1.3 %collective-permute-start.1 = (bf16[2,4,16,2048]{3,2,1,0:T(8,128)(2,1)S(1)}, bf16[2,4,16,2048]{3,2,1,0:T(8,128)(2,1)S(1)}, u32[]{:S(2)}, u32[]{:S(2)}) collective-permute-start(bf16[2,4,16,2048]{3,2,1,0:T(8,128)(2,1)S(1)} %get-tuple-element.39), channel_id=1, source_target_pairs={{1,0},{2,1},{3,2},{4,3},{5,4},{6,5},{7,6},{9,8},{10,9},{11,10},{12... | collective-permute-start | bytes 1572872 | tf_op jit(solution)/shard_map/ppermute | solution.py:24
  5.7 0.0 copy-done.4
  5.7 0.5 slice_reduce_fusion.32
  6.2 0.4 slice_reduce_fusion.31
  7.8 1.2 %select_convert_fusion.1 = bf16[4,160,128]{2,1,0:T(8,128)(2,1)S(1)} fusion(bf16[4]{0:T(256)(128)(2,1)S(1)} %get-tuple-element.37, bf16[4]{0:T(256)(128)(2,1)S(1)} %get-tuple-element.38, bf16[4]{0:T(256)(128)(2,1)S(1)} %get-tuple-element.7, bf16[4]{0:T(256)(128)(2,1)S(1)} %get-tuple-element.8, bf16[4]{0:T(256)(128)(2,1)S(1)} %get-tuple-element.9, ...), kind=kLoop, calls=%fused_computation.15 | loop fusion | flops 2703360 | bytes 839944 | tf_op jit(solution)/shard_map/convert_element_type | solution.py:41
  9.0 1.0 %fusion.14.cols_ref = bf16[4,512,256]{2,1,0:T(8,128)(2,1)} fusion(bf16[4,160,128]{2,1,0:T(8,128)(2,1)S(1)} %select_convert_fusion.1), kind=kLoop, calls=%fused_computation.12 | loop fusion | flops 4194304 | bytes 1212416 | tf_op jit(solution)/shard_map/concatenate | solution.py:48
  10.1 0.0 copy-done.3
  10.1 0.6 select_reduce_fusion.order_ref
  10.7 2.5 %select_convert_fusion.rows_ref = bf16[4,128,160]{2,1,0:T(8,128)(2,1)} fusion(bf16[4]{0:T(256)(128)(2,1)S(1)} %get-tuple-element.37, bf16[4]{0:T(256)(128)(2,1)S(1)} %get-tuple-element.38, bf16[4]{0:T(256)(128)(2,1)S(1)} %get-tuple-element.7, bf16[4]{0:T(256)(128)(2,1)S(1)} %get-tuple-element.8, bf16[4]{0:T(256)(128)(2,1)S(1)} %get-tuple-element.9, ...), kind=kLoop, calls=%fused_computation.14 | loop fusion | flops 2703360 | bytes 839944 | tf_op jit(solution)/shard_map/convert_element_type | solution.py:41
  13.2 0.0 collective-permute-done.before_ref
  13.3 0.0 copy-start.6
  13.3 0.0 collective-permute-done.1.after_ref
  13.3 0.0 copy-start.7
  13.3 0.8 copy-done.6
  14.0 0.2 copy-done.7
  14.2 19.9 %column_products.1 = bf16[8,2,256,128]{3,2,1,0:T(8,128)(2,1)} custom-call(s32[8]{0:T(128)} %select_reduce_fusion.order_ref, bf16[2,4,256,2048]{3,2,1,0:T(8,128)(2,1)} %bitcast.38, bf16[2,4,16,2048]{3,2,1,0:T(8,128)(2,1)} %copy-done.6, bf16[2,4,16,2048]{3,2,1,0:T(8,128)(2,1)} %copy-done.7, bf16[4,128,160]{2,1,0:T(8,128)(2,1)} %select_convert_fusion.rows_ref, ...), custom_call_target="tpu_custom_call" | custom-call | tf_op jit(solution)/shard_map/column_products/pallas_call | solution.py:114
  34.2 0.0 copy-start.5
  34.2 9.4 %all-to-all-start = ((bf16[8,2,256,128]{3,2,1,0:T(8,128)(2,1)}), bf16[8,2,256,128]{3,2,1,0:T(8,128)(2,1)S(1)}, u32[]{:S(2)}, u32[]{:S(2)}) async-start(bf16[8,2,256,128]{3,2,1,0:T(8,128)(2,1)} %column_products.1), calls=%async_computation | async-start | bytes 2097152 | tf_op jit(solution)/shard_map/all_to_all | solution.py:289
  43.6 0.0 copy-done.5
  43.6 2.1 %reshape_squeeze.3 = bf16[8,256,4,128]{3,2,1,0:T(4,128)(2,1)} reshape(bf16[1,2048,512]{2,1,0:T(8,128)(2,1)S(1)} %copy-done.5) | data formatting | bytes 4194304 | tf_op jit(solution)/shard_map/reshape;squeeze | solution.py:290
  45.7 0.6 gather_fusion
  46.3 0.1 select_reduce_fusion.1
  46.5 12.5 %all-to-all-done = bf16[8,2,256,128]{3,2,1,0:T(8,128)(2,1)S(1)} async-done(((bf16[8,2,256,128]{3,2,1,0:T(8,128)(2,1)}), bf16[8,2,256,128]{3,2,1,0:T(8,128)(2,1)S(1)}, u32[]{:S(2)}, u32[]{:S(2)}) %all-to-all-start) | async-done | bytes 1048608 | tf_op jit(solution)/shard_map/all_to_all | solution.py:289
  58.9 2.4 %fusion.11 = bf16[4,2,128,128]{2,3,0,1:T(8,128)(2,1)S(1)} fusion(bf16[8,256,4,128]{3,2,1,0:T(4,128)(2,1)} %reshape_squeeze.3, bf16[8,2,256,128]{3,2,1,0:T(8,128)(2,1)S(1)} %all-to-all-done), kind=kOutput, calls=%fused_computation.11 | convolution fusion | flops 537001984 | bytes 3407872 | tf_op jit(solution)/shard_map/xrai,xcrj->acij/dot_general | solution.py:291
  61.3 0.0 copy-start.9
  61.3 0.0 copy-start.10
  61.3 0.0 copy-start
  61.3 0.0 copy-start.1
  61.4 0.0 copy-start.2
  61.4 0.0 copy-start.8
  61.4 0.2 copy.24
  61.6 0.6 gather_fusion.1
  62.2 0.8 broadcast_select_fusion
  63.0 4.9 %all-to-all-start.1 = ((bf16[4,2,128,128]{3,2,1,0:T(8,128)(2,1)}), bf16[4,2,128,128]{3,2,1,0:T(8,128)(2,1)S(1)}, u32[]{:S(2)}, u32[]{:S(2)}) async-start(bf16[4,2,128,128]{3,2,1,0:T(8,128)(2,1)} %broadcast_select_fusion), calls=%async_computation.1 | async-start | bytes 524288 | tf_op jit(solution)/shard_map/all_to_all | solution.py:295
  67.8 0.0 copy-done.9
  67.8 0.1 copy.25.corner_ref
  67.9 0.0 copy-done.10
  67.9 0.2 convert_reduce_fusion
  68.1 6.5 %all-to-all-done.1.mine_ref = bf16[4,2,128,128]{3,2,1,0:T(8,128)(2,1)S(1)} async-done(((bf16[4,2,128,128]{3,2,1,0:T(8,128)(2,1)}), bf16[4,2,128,128]{3,2,1,0:T(8,128)(2,1)S(1)}, u32[]{:S(2)}, u32[]{:S(2)}) %all-to-all-start.1) | async-done | bytes 262176 | tf_op jit(solution)/shard_map/all_to_all | solution.py:295
  74.6 0.0 copy-done
  74.6 0.0 copy-done.1
  74.6 0.0 copy-done.2
  74.6 9.5 %formed_and_predicted.1 = (bf16[2,512,512]{2,1,0:T(8,128)(2,1)}, bf16[128,2,128]{2,1,0:T(2,128)(2,1)}) custom-call(s32[64,2]{1,0:T(8,128)S(1)} %copy.25.corner_ref, s32[64]{0:T(128)S(1)} %multiply_add_fusion.target_ref, bf16[4,2,128,128]{3,2,1,0:T(8,128)(2,1)S(1)} %all-to-all-done.1.mine_ref, bf16[4,512,128]{2,1,0:T(8,128)(2,1)S(1)} %copy-done, ...), custom_call_target="tpu_custom_call" | custom-call | tf_op jit(solution)/shard_map/formed_and_predicted/pallas_call | solution.py:237
  84.1 4.2 %all-to-all-start.2 = ((bf16[32,4,2,128]{3,2,1,0:T(2,128)(2,1)}), bf16[32,4,2,128]{3,2,1,0:T(2,128)(2,1)S(1)}, u32[]{:S(2)}, u32[]{:S(2)}) async-start(bf16[32,4,2,128]{3,2,1,0:T(2,128)(2,1)} %bitcast.12), calls=%async_computation.2 | async-start | bytes 131072 | tf_op jit(solution)/shard_map/all_to_all | solution.py:309
  88.3 3.3 %gain_products.1 = f32[128,2,128]{2,1,0:T(2,128)} custom-call(f32[2,512]{1,0:T(2,128)} %gains_ref.1, s32[128,2,128]{2,1,0:T(2,128)} %index_ref.1), custom_call_target="tpu_custom_call" | custom-call | tf_op jit(solution)/shard_map/gain_products/pallas_call | solution.py:161
  91.6 4.1 %all-to-all-done.2 = bf16[32,4,2,128]{3,2,1,0:T(2,128)(2,1)S(1)} async-done(((bf16[32,4,2,128]{3,2,1,0:T(2,128)(2,1)}), bf16[32,4,2,128]{3,2,1,0:T(2,128)(2,1)S(1)}, u32[]{:S(2)}, u32[]{:S(2)}) %all-to-all-start.2) | async-done | bytes 65568 | tf_op jit(solution)/shard_map/all_to_all | solution.py:309
  95.7 0.0 copy-done.8
  95.7 1.7 %fusion.16 = f32[128,2,128]{2,1,0:T(2,128)} fusion(f32[128,2,128]{2,1,0:T(2,128)S(1)} %copy-done.8, f32[128,2,128]{2,1,0:T(2,128)} %gain_products.1, bf16[32,4,2,128]{3,2,1,0:T(2,128)(2,1)S(1)} %all-to-all-done.2), kind=kLoop, calls=%fused_computation.18 | loop fusion | flops 98304 | bytes 458752 | tf_op jit(solution)/shard_map/sub | solution.py:314
  (42 shorter events, 1.0 us)
Async XLA Ops:
  0.6 5.1 %copy-start.4 = (f32[4,33]{1,0:T(4,128)S(1)}, f32[4,33]{1,0:T(4,128)}, u32[]{:S(2)}) copy-start(f32[4,33]{1,0:T(4,128)} %param.14) | copy-start | bytes 1588
  2.0 8.1 %copy-start.3 = (s32[32]{0:T(128)S(1)}, s32[32]{0:T(128)}, u32[]{:S(2)}) copy-start(s32[32]{0:T(128)} %param.19) | copy-start | bytes 388
  2.0 11.3 %collective-permute-start = (bf16[2,4,16,2048]{3,2,1,0:T(8,128)(2,1)S(1)}, bf16[2,4,16,2048]{3,2,1,0:T(8,128)(2,1)S(1)}, u32[]{:S(2)}, u32[]{:S(2)}) collective-permute-start(bf16[2,4,16,2048]{3,2,1,0:T(8,128)(2,1)S(1)} %get-tuple-element.40), channel_id=1, source_target_pairs={{0,1},{1,2},{2,3},{3,4},{4,5},{5,6},{6,7},{8,9},{9,10},{10,11},{11... | collective-permute-start | bytes 1572872 | tf_op jit(solution)/shard_map/ppermute | solution.py:24
  4.4 8.9 %collective-permute-start.1 = (bf16[2,4,16,2048]{3,2,1,0:T(8,128)(2,1)S(1)}, bf16[2,4,16,2048]{3,2,1,0:T(8,128)(2,1)S(1)}, u32[]{:S(2)}, u32[]{:S(2)}) collective-permute-start(bf16[2,4,16,2048]{3,2,1,0:T(8,128)(2,1)S(1)} %get-tuple-element.39), channel_id=1, source_target_pairs={{1,0},{2,1},{3,2},{4,3},{5,4},{6,5},{7,6},{9,8},{10,9},{11,10},{12... | collective-permute-start | bytes 1572872 | tf_op jit(solution)/shard_map/ppermute | solution.py:24
  13.3 0.8 copy-start.6
  13.3 1.0 %copy-start.7 = (bf16[2,4,16,2048]{3,2,1,0:T(8,128)(2,1)}, bf16[2,4,16,2048]{3,2,1,0:T(8,128)(2,1)S(1)}, u32[]{:S(2)}) copy-start(bf16[2,4,16,2048]{3,2,1,0:T(8,128)(2,1)S(1)} %collective-permute-done.1.after_ref) | copy-start | bytes 1572868
  34.2 9.4 %copy-start.5 = (bf16[1,2048,512]{2,1,0:T(8,128)(2,1)S(1)}, bf16[1,2048,512]{2,1,0:T(8,128)(2,1)}, u32[]{:S(2)}) copy-start(bf16[1,2048,512]{2,1,0:T(8,128)(2,1)} %param.15) | copy-start | bytes 6291460
  34.2 24.8 %all-to-all-start = ((bf16[8,2,256,128]{3,2,1,0:T(8,128)(2,1)}), bf16[8,2,256,128]{3,2,1,0:T(8,128)(2,1)S(1)}, u32[]{:S(2)}, u32[]{:S(2)}) async-start(bf16[8,2,256,128]{3,2,1,0:T(8,128)(2,1)} %column_products.1), calls=%async_computation | async-start | bytes 2097152 | tf_op jit(solution)/shard_map/all_to_all | solution.py:289
  61.3 6.5 %copy-start.9 = (s32[64,2]{0,1:T(2,128)S(1)}, s32[64,2]{0,1:T(2,128)}, u32[]{:S(2)}) copy-start(s32[64,2]{0,1:T(2,128)} %param.20) | copy-start | bytes 1540
  61.3 6.6 %copy-start.10 = (s32[64,1]{0,1:T(1,128)S(1)}, s32[64,1]{0,1:T(1,128)}, u32[]{:S(2)}) copy-start(s32[64,1]{0,1:T(1,128)} %param.22) | copy-start | bytes 772
  61.3 13.3 %copy-start = (bf16[4,512,128]{2,1,0:T(8,128)(2,1)S(1)}, bf16[4,512,128]{2,1,0:T(8,128)(2,1)}, u32[]{:S(2)}) copy-start(bf16[4,512,128]{2,1,0:T(8,128)(2,1)} %cols_ref.1) | copy-start | bytes 1572868
  61.3 13.3 %copy-start.1 = (bf16[4,512,128]{2,1,0:T(8,128)(2,1)S(1)}, bf16[4,512,128]{2,1,0:T(8,128)(2,1)}, u32[]{:S(2)}) copy-start(bf16[4,512,128]{2,1,0:T(8,128)(2,1)} %rows_ref.1) | copy-start | bytes 1572868
  61.4 13.3 %copy-start.2 = (f32[64,2,128]{2,1,0:T(2,128)S(1)}, f32[64,2,128]{2,1,0:T(2,128)}, u32[]{:S(2)}) copy-start(f32[64,2,128]{2,1,0:T(2,128)} %offset_ref.1) | copy-start | bytes 196612
  61.4 34.3 %copy-start.8 = (f32[128,2,128]{2,1,0:T(2,128)S(1)}, f32[128,2,128]{2,1,0:T(2,128)}, u32[]{:S(2)}) copy-start(f32[128,2,128]{2,1,0:T(2,128)} %param.23) | copy-start | bytes 393220
  63.0 11.6 %all-to-all-start.1 = ((bf16[4,2,128,128]{3,2,1,0:T(8,128)(2,1)}), bf16[4,2,128,128]{3,2,1,0:T(8,128)(2,1)S(1)}, u32[]{:S(2)}, u32[]{:S(2)}) async-start(bf16[4,2,128,128]{3,2,1,0:T(8,128)(2,1)} %broadcast_select_fusion), calls=%async_computation.1 | async-start | bytes 524288 | tf_op jit(solution)/shard_map/all_to_all | solution.py:295
  84.1 11.6 %all-to-all-start.2 = ((bf16[32,4,2,128]{3,2,1,0:T(2,128)(2,1)}), bf16[32,4,2,128]{3,2,1,0:T(2,128)(2,1)S(1)}, u32[]{:S(2)}, u32[]{:S(2)}) async-start(bf16[32,4,2,128]{3,2,1,0:T(2,128)(2,1)} %bitcast.12), calls=%async_computation.2 | async-start | bytes 131072 | tf_op jit(solution)/shard_map/all_to_all | solution.py:309

commit v3 on v2

--- a/solution.py
+++ b/solution.py
@@ -1,3 +1,5 @@
+import functools
+
 import jax
 import jax.numpy as jnp
 from jax import lax
@@ -13,129 +15,170 @@
 
 LANES = 128
 COL_TILE = 256
-
-
-def halo_rows(x, axis, dim, width):
-    count, length = (lax.axis_size(axis), x.shape[dim])
-    up = [(i, (i + 1) % count) for i in range(count - 1)]
-    down = [(j, i) for i, j in up]
-    last = lax.slice_in_dim(x, length - width, length, axis=dim)
-    initial = lax.slice_in_dim(x, 0, width, axis=dim)
-    return lax.ppermute(last, axis, up), lax.ppermute(initial, axis, down)
-
-
-def band_matrices(kernels):
-    taps = kernels.shape[1]
-    width = (taps - 1) // 2
+MESH = pl.DeviceIdType.MESH
+
+
+def fill_bands(taps_ref, across_ref, down_ref, width):
+    scales, taps = taps_ref.shape
     span = LANES + taps - 1
     k = lax.broadcasted_iota(jnp.int32, (span, LANES), 0)
     n = lax.broadcasted_iota(jnp.int32, (span, LANES), 1)
     i = lax.broadcasted_iota(jnp.int32, (LANES, span), 0)
     m = lax.broadcasted_iota(jnp.int32, (LANES, span), 1)
-    down = jnp.zeros((kernels.shape[0], span, LANES), jnp.float32)
-    across = jnp.zeros((kernels.shape[0], LANES, span), jnp.float32)
-    for t in range(taps):
-        tap = kernels[:, t][:, None, None]
-        down = jnp.where((k - n == t)[None], tap, down)
-        across = jnp.where((m - i == t)[None], tap, across)
-    down, across = down.astype(jnp.bfloat16), across.astype(jnp.bfloat16)
-    tiles = COL_TILE // LANES
-    window = COL_TILE + 2 * LANES
-    pieces = []
-    for tile in range(tiles):
-        start = LANES - width + tile * LANES
-        pieces.append(jnp.pad(down, ((0, 0), (start, window - start - span), (0, 0))))
-    return across, jnp.concatenate(pieces, axis=2)
-
-
-def smooth_kernel(order_ref, x_ref, before_ref, after_ref, rows_ref, cols_ref, taper_ref, out_ref, y_ref, acc_ref):
-    step = pl.program_id(0)
-    tiles = pl.num_programs(0) - 1
-    corr, scales, rows = x_ref.shape[0], x_ref.shape[1], x_ref.shape[2]
-    width = before_ref.shape[2]
-    targets = out_ref.shape[0]
-
-    @pl.when(step == 0)
-    def _():
-        y_ref[:, :, 0:COL_TILE] = jnp.zeros((scales, corr * rows, COL_TILE), y_ref.dtype)
-        acc_ref[...] = jnp.zeros_like(acc_ref)
-
-    lane = pl.multiple_of((step + 1) * COL_TILE, COL_TILE)
-
-    @pl.when(step == tiles)
-    def _():
-        y_ref[:, :, pl.ds(lane, COL_TILE)] = jnp.zeros((scales, corr * rows, COL_TILE), y_ref.dtype)
-
-    @pl.when(step < tiles)
-    def _():
-        for c in range(corr):
+    down_ref[...] = jnp.zeros_like(down_ref)
+    for s in range(scales):
+
+        def one_tap(t, carry, s=s):
+            down, across = carry
+            tap = taps_ref[s, t]
+            return jnp.where(k - n == t, tap, down), jnp.where(m - i == t, tap, across)
+
+        down, across = lax.fori_loop(
+            0,
+            taps,
+            one_tap,
+            (jnp.zeros((span, LANES), jnp.float32), jnp.zeros((LANES, span), jnp.float32)),
+            unroll=3,
+        )
+        across_ref[s] = across.astype(across_ref.dtype)
+        down = down.astype(down_ref.dtype)
+        for tile in range(COL_TILE // LANES):
+            start = LANES - width + tile * LANES
+            down_ref[s, start : start + span, tile * LANES : (tile + 1) * LANES] = down
+
+
+def smooth_kernel(count, order_ref, taps_ref, x_ref, taper_in, out_ref, x_buf, taper_ref, across_ref, down_ref, y_ref, smooth_ref, acc_ref, stage_ref, local_sem, taper_sem, halo_send, halo_recv, send_sem, recv_sem):
+    corr, scales, rows, side = x_ref.shape
+    width = (taps_ref.shape[1] - 1) // 2
+    tiles = side // COL_TILE
+    me = lax.axis_index("strip")
+    right, left = lax.rem(me + 1, count), lax.rem(me + count - 1, count)
+    loads = [
+        pltpu.make_async_copy(x_ref.at[c], x_buf.at[c, :, pl.ds(width, rows)], local_sem.at[c])
+        for c in range(corr)
+    ]
+    taper_load = pltpu.make_async_copy(taper_in, taper_ref, taper_sem)
+    for load in loads:
+        load.start()
+    taper_load.start()
+    barrier = pltpu.get_barrier_semaphore()
+    for off in range(1, count):
+        pl.semaphore_signal(
+            barrier, inc=1, device_id={"strip": lax.rem(me + off, count)}, device_id_type=MESH
+        )
+    pl.semaphore_wait(barrier, count - 1)
+    halos = []
+    for c in range(corr):
+        pair = []
+        for way, (start, landing, peer) in enumerate(
+            ((rows - width, 0, right), (0, rows + width, left))
+        ):
+            pair.append(
+                pltpu.make_async_remote_copy(
+                    src_ref=x_ref.at[c, :, pl.ds(start, width)],
+                    dst_ref=x_buf.at[c, :, pl.ds(landing, width)],
+                    send_sem=halo_send.at[c, way],
+                    recv_sem=halo_recv.at[c, way],
+                    device_id={"strip": peer},
+                    device_id_type=MESH,
+                )
+            )
+        for copy in pair:
+            copy.start()
+        halos.append(pair)
+    fill_bands(taps_ref, across_ref, down_ref, width)
+    y_ref[:, :, 0:LANES] = jnp.zeros((scales, rows, LANES), y_ref.dtype)
+    y_ref[:, :, LANES + side : 2 * LANES + side] = jnp.zeros((scales, rows, LANES), y_ref.dtype)
+    sends = []
+    for c in range(corr):
+        loads[c].wait()
+        for copy in halos[c]:
+            copy.wait()
+
+        @pl.when(me == 0)
+        def _():
+            x_buf[c, :, 0:width] = jnp.zeros((scales, width, side), x_buf.dtype)
+
+        @pl.when(me == count - 1)
+        def _():
+            x_buf[c, :, rows + width : rows + 2 * width] = jnp.zeros((scales, width, side), x_buf.dtype)
+
+        for s in range(scales):
+            for b in range(rows // LANES):
+                part = x_buf[c, s, b * LANES : (b + 1) * LANES + 2 * width]
+                y = jnp.dot(across_ref[s], part, preferred_element_type=jnp.float32)
+                y_ref[s, b * LANES : (b + 1) * LANES, LANES : LANES + side] = y.astype(y_ref.dtype)
+
+        def one_tile(tile, carry):
+            first = pl.multiple_of(tile * COL_TILE, COL_TILE)
+            smoothed = jnp.zeros((rows, COL_TILE), jnp.float32)
             for s in range(scales):
-                full = jnp.concatenate([before_ref[c, s], x_ref[c, s], after_ref[c, s]], axis=0)
-                for b in range(rows // LANES):
-                    part = full[b * LANES : (b + 1) * LANES + 2 * width]
-                    y = jnp.dot(rows_ref[s], part, preferred_element_type=jnp.float32)
-                    at = c * rows + b * LANES
-                    y_ref[s, at : at + LANES, pl.ds(lane, COL_TILE)] = y.astype(y_ref.dtype)
-
-    @pl.when(step > 0)
-    def _():
-        first = pl.multiple_of(step * COL_TILE - LANES, LANES)
-        smoothed = jnp.zeros((corr * rows, COL_TILE), jnp.float32)
-        for s in range(scales):
-            smoothed += jnp.dot(
-                y_ref[s, :, pl.ds(first, COL_TILE + 2 * LANES)],
-                cols_ref[s],
-                preferred_element_type=jnp.float32,
+                smoothed += jnp.dot(
+                    y_ref[s, :, pl.ds(first, COL_TILE + 2 * LANES)],
+                    down_ref[s],
+                    preferred_element_type=jnp.float32,
+                )
+            smooth_ref[:, pl.ds(first, COL_TILE)] = smoothed.astype(smooth_ref.dtype)
+            return carry
+
+        lax.fori_loop(0, tiles, one_tile, 0, unroll=2)
+        if c == 0:
+            taper_load.wait()
+        acc = jnp.dot(smooth_ref[...], taper_ref[...], preferred_element_type=jnp.float32)
+        for d in range(count):
+            acc_ref[d] = acc[:, d * LANES : (d + 1) * LANES]
+        for d in range(count):
+            stage_ref[c, d] = acc_ref[order_ref[d]].astype(stage_ref.dtype)
+        for off in range(1, count):
+            peer = lax.rem(me + off, count)
+            copy = pltpu.make_async_remote_copy(
+                src_ref=stage_ref.at[c, peer],
+                dst_ref=out_ref.at[me, c],
+                send_sem=send_sem.at[c, off],
+                recv_sem=recv_sem.at[c, off],
+                device_id={"strip": peer},
+                device_id_type=MESH,
             )
-        acc_ref[...] += jnp.dot(
-            smoothed.astype(jnp.bfloat16), taper_ref[...], preferred_element_type=jnp.float32
-        )
-
-    @pl.when(step == tiles)
-    def _():
-        for d in range(targets):
-            at = pl.multiple_of(order_ref[d] * LANES, LANES)
-            for c in range(corr):
-                out_ref[d, c] = acc_ref[c * rows : (c + 1) * rows, pl.ds(at, LANES)].astype(out_ref.dtype)
-
-
-def column_products(comp, before, after, kernels, taper, order):
+            copy.start()
+            sends.append(copy)
+        out_ref[me, c] = stage_ref[c, me]
+    for copy in sends:
+        copy.wait()
+
+
+def regrouped_products(comp, kernels, taper, order):
     corr, scales, rows, side = comp.shape
-    width = before.shape[2]
-    across, down = band_matrices(kernels)
-    tiles = side // COL_TILE
-    wide = taper.shape[1]
-    targets = wide // LANES
-    last = tiles - 1
-
-    def ahead(j, order):
-        return (0, 0, 0, jnp.minimum(j, last))
-
+    taps = kernels.shape[1]
+    count = lax.axis_size("strip")
+    whole = pl.BlockSpec(memory_space=pltpu.VMEM)
+    scalars = pl.BlockSpec(memory_space=pltpu.SMEM)
+    remote = pl.BlockSpec(memory_space=pl.ANY)
     return pl.pallas_call(
-        smooth_kernel,
-        grid_spec=pltpu.PrefetchScalarGridSpec(
-            num_scalar_prefetch=1,
-            grid=(tiles + 1,),
-            in_specs=[
-                pl.BlockSpec((corr, scales, rows, COL_TILE), ahead),
-                pl.BlockSpec((corr, scales, width, COL_TILE), ahead),
-                pl.BlockSpec((corr, scales, width, COL_TILE), ahead),
-                pl.BlockSpec(across.shape, lambda j, order: (0, 0, 0)),
-                pl.BlockSpec(down.shape, lambda j, order: (0, 0, 0)),
-                pl.BlockSpec((COL_TILE, wide), lambda j, order: (jnp.maximum(j - 1, 0), 0)),
-            ],
-            out_specs=pl.BlockSpec((targets, corr, rows, LANES), lambda j, order: (0, 0, 0, 0)),
-            scratch_shapes=[
-                pltpu.VMEM((scales, corr * rows, side + 2 * COL_TILE), jnp.bfloat16),
-                pltpu.VMEM((corr * rows, wide), jnp.float32),
-            ],
+        functools.partial(smooth_kernel, count),
+        in_specs=[scalars, scalars, remote, remote],
+        out_specs=whole,
+        scratch_shapes=[
+            pltpu.VMEM((corr, scales, rows + taps - 1, side), jnp.bfloat16),
+            pltpu.VMEM(taper.shape, jnp.bfloat16),
+            pltpu.VMEM((scales, LANES, LANES + taps - 1), jnp.bfloat16),
+            pltpu.VMEM((scales, COL_TILE + 2 * LANES, COL_TILE), jnp.bfloat16),
+            pltpu.VMEM((scales, rows, side + 2 * LANES), jnp.bfloat16),
+            pltpu.VMEM((rows, side), jnp.bfloat16),
+            pltpu.VMEM((count, rows, LANES), jnp.float32),
+            pltpu.VMEM((corr, count, rows, LANES), jnp.bfloat16),
+            pltpu.SemaphoreType.DMA((corr,)),
+            pltpu.SemaphoreType.DMA,
+            pltpu.SemaphoreType.DMA((corr, 2)),
+            pltpu.SemaphoreType.DMA((corr, 2)),
+            pltpu.SemaphoreType.DMA((corr, count)),
+            pltpu.SemaphoreType.DMA((corr, count)),
+        ],
+        out_shape=jax.ShapeDtypeStruct((count, corr, rows, LANES), jnp.bfloat16),
+        compiler_params=pltpu.CompilerParams(
+            collective_id=0, has_side_effects=True, vmem_limit_bytes=60 * 1024 * 1024
         ),
-        out_shape=jax.ShapeDtypeStruct((targets, corr, rows, LANES), jnp.bfloat16),
-        compiler_params=pltpu.CompilerParams(
-            dimension_semantics=("arbitrary",), vmem_limit_bytes=60 * 1024 * 1024
-        ),
-        name="column_products",
-    )(order, comp, before, after, across, down, taper)
+        name="regrouped_products",
+    )(order, kernels, comp, taper)
 
 
 def looked_up(row, index):
@@ -279,14 +322,11 @@
     contrib_side = finish_cols.shape[2]
     sub_rows = row_taper.shape[2] // contrib_side
     sub_cols = col_taper.shape[2] // contrib_side
-    width = (scale_kernels.shape[1] - 1) // 2
-    before, after = halo_rows(comp, "strip", 2, width)
     col_perm = subgrid_owner[:sub_cols] % n_strip
     row_perm = subgrid_owner[jnp.arange(sub_rows, dtype=jnp.int32) * sub_cols] // n_strip
     col_inverse = inverse_of(col_perm)
     row_inverse = inverse_of(row_perm)
-    by_target = column_products(comp, before, after, scale_kernels, col_taper[0], col_inverse)
-    regrouped = lax.all_to_all(by_target, "strip", split_axis=0, concat_axis=0, tiled=True)
+    regrouped = regrouped_products(comp, scale_kernels, col_taper[0], col_inverse)
     all_rows = row_taper[0].reshape(n_strip, rows, sub_rows, contrib_side)
     finished = jnp.einsum(
         "xrai,xcrj->acij", all_rows, regrouped, preferred_element_type=jnp.float32

time: 97.8 us -> 77.8 us (0.80)
  starting transfers between devices: 22.1 us -> 7.74 us
  Pallas kernels: 32.7 us -> 44 us
  waiting for transfers between devices: 23.1 us -> 14 us
  other arithmetic: 9.16 us -> 4.08 us
  local copies, waits for them, and re-layouts: 6.85 us -> 4.76 us
    all_to_all x1 -> x0, waiting for transfers between devices: 12.5 us -> none  [on_device(): lax.all_to_all(by_target, 'strip', split_axis=0, concat_axis=0, tiled=True)]
    pallas_call x1, Pallas kernels: 19.9 us -> 31.3 us  [regrouped_products(): pl.pallas_call(functools.partial(smooth_kernel, count), in_specs=[scalars...]
    all_to_all x1 -> x0, starting transfers between devices: 9.4 us -> none  [on_device(): lax.all_to_all(by_target, 'strip', split_axis=0, concat_axis=0, tiled=True)]
    ppermute x2 -> x0, starting transfers between devices: 3.72 us -> none  [halo_rows(): return (lax.ppermute(last, axis, up), lax.ppermute(initial, axis, down))]
    convert_element_type x2 -> x0, other arithmetic: 3.72 us -> none  [band_matrices(): down, across = (down.astype(jnp.bfloat16), across.astype(jnp.bfloat16))]
    all_to_all x1, waiting for transfers between devices: 6.49 us -> 9.87 us  [on_device(): lax.all_to_all(outgoing, 'facet', split_axis=0, concat_axis=0, tiled=True)]
    slice x3 -> x0, local copies, waits for them, and re-layouts: 2.22 us -> none  [the longest x1 1.31 us: halo_rows(): initial = lax.slice_in_dim(x, 0, width, axis=dim)]
    all_to_all x1, starting transfers between devices: 4.17 us -> 2.87 us  [on_device(): lax.all_to_all(outgoing_vis, ('facet', 'strip'), split_axis=0, concat_axi...]
  transfers between devices with their start and end apart: 5 -> 2, of which waited for: 3 -> 2; matrix products, arithmetic and copies ran while one was open for 11% -> 0% of each run, Pallas kernels for 3% -> 4%
where the time goes in v3:
time: 77.8 us; the launch traced here: 77.4 us
  Pallas kernels  44 us (57%)
  waiting for transfers between devices  14 us (18%)
  starting transfers between devices  7.74 us (10%)
  local copies, waits for them, and re-layouts  4.76 us (6%)
  other arithmetic  4.08 us (5%)
  matrix products  1.96 us (3%)
    pallas_call x1, Pallas kernels, regrouped_products(): pl.pallas_call(functools.partial(smooth_kernel, count), in_specs=[scalars...  31.3 us
    all_to_all x1, waiting for transfers between devices, on_device(): lax.all_to_all(outgoing, 'facet', split_axis=0, concat_axis=0, tiled=True)  9.87 us
    pallas_call x1, Pallas kernels, formed_and_predicted(): pl.pallas_call(degrid_kernel, in_specs=[scalars, scalars, whole, whole, w...  9.5 us
    all_to_all x1, starting transfers between devices, on_device(): lax.all_to_all(outgoing, 'facet', split_axis=0, concat_axis=0, tiled=True)  4.87 us
    all_to_all x1, waiting for transfers between devices, on_device(): lax.all_to_all(outgoing_vis, ('facet', 'strip'), split_axis=0, concat_axi...  4.15 us
    pallas_call x1, Pallas kernels, gain_products(): pl.pallas_call(gain_kernel, grid=(rows // step,), in_specs=[pl.BlockSpec(...  3.26 us
    all_to_all x1, starting transfers between devices, on_device(): lax.all_to_all(outgoing_vis, ('facet', 'strip'), split_axis=0, concat_axi...  2.87 us
    another operation x1, local copies, waits for them, and re-layouts, on_device(): all_rows = row_taper[0].reshape(n_strip, rows, sub_rows, contrib_side)  2.55 us
  transfers between devices with their start and end apart: 2, of which 2 were waited for; matrix products, arithmetic and copies ran while one was open for 0% of the time, Pallas kernels for 4%

profile of v3, /device:TPU:0, one launch (start us, length us, event | category | flops | bytes accessed | tf_op | source)
XLA Modules:
  0.0 77.4 jit_solution(13751357293928508594)
XLA Ops:
  0.7 0.7 and_select_fusion
  1.3 1.3 %gather_fusion = s32[4]{0:T(128)S(1)} fusion(s32[32]{0:T(128)} %param.19, s32[1024]{0:T(1024)S(1)} %pad_clamp_fusion.1), kind=kCustom, calls=%fused_computation | custom fusion | bytes 48 | tf_op jit(solution)/shard_map/gather | solution.py:326
  2.6 0.1 select_reduce_fusion.1
  2.8 2.6 %reshape_squeeze.3 = bf16[8,256,4,128]{3,2,1,0:T(4,128)(2,1)S(1)} reshape(bf16[1,2048,512]{2,1,0:T(8,128)(2,1)} %param.15) | data formatting | bytes 4194304 | tf_op jit(solution)/shard_map/reshape;squeeze | solution.py:330
  5.3 0.6 select_reduce_fusion.order_ref
  6.0 31.3 %regrouped_products.1 = bf16[8,2,256,128]{3,2,1,0:T(8,128)(2,1)} custom-call(s32[8]{0:T(128)} %select_reduce_fusion.order_ref, f32[4,33]{1,0:T(4,128)} %taps_ref.1, bf16[2,4,256,2048]{3,2,1,0:T(8,128)(2,1)} %bitcast.37, bf16[2048,1024]{1,0:T(8,128)(2,1)} %bitcast.38), custom_call_target="tpu_custom_call" | custom-call | tf_op jit(solution)/shard_map/regrouped_products/pallas_call | solution.py:156
  37.3 2.0 %fusion.9 = bf16[4,2,128,128]{2,3,0,1:T(8,128)(2,1)S(1)} fusion(bf16[8,256,4,128]{3,2,1,0:T(4,128)(2,1)S(1)} %reshape_squeeze.3, bf16[8,2,256,128]{3,2,1,0:T(8,128)(2,1)} %regrouped_products.1), kind=kOutput, calls=%fused_computation.7 | convolution fusion | flops 537001984 | bytes 3407872 | tf_op jit(solution)/shard_map/xrai,xcrj->acij/dot_general | solution.py:331
  39.2 0.0 copy-start.4
  39.2 0.0 copy-start.5
  39.3 0.0 copy-start
  39.3 0.0 copy-start.1
  39.3 0.0 copy-start.2
  39.3 0.0 copy-start.3
  39.3 0.2 copy.24
  39.5 0.6 gather_fusion.1
  40.1 0.8 %broadcast_select_fusion = bf16[4,2,128,128]{3,2,1,0:T(8,128)(2,1)} fusion(bf16[4,2,128,128]{3,2,1,0:T(8,128)(2,1)S(1)} %gather_fusion.1, pred[4]{0:T(512)(128)(4,1)S(1)} %compare_and_fusion), kind=kLoop, calls=%fused_computation.9 | loop fusion | flops 131072 | bytes 524292 | tf_op jit(solution)/shard_map/jit(_take)/select_n | solution.py:334
  40.9 4.9 %all-to-all-start = ((bf16[4,2,128,128]{3,2,1,0:T(8,128)(2,1)}), bf16[4,2,128,128]{3,2,1,0:T(8,128)(2,1)S(1)}, u32[]{:S(2)}, u32[]{:S(2)}) async-start(bf16[4,2,128,128]{3,2,1,0:T(8,128)(2,1)} %broadcast_select_fusion), calls=%async_computation | async-start | bytes 524288 | tf_op jit(solution)/shard_map/all_to_all | solution.py:335
  45.8 0.0 copy-done.4
  45.8 0.1 copy.25.corner_ref
  45.9 0.0 copy-done.5
  45.9 0.2 convert_reduce_fusion
  46.0 9.9 %all-to-all-done.mine_ref = bf16[4,2,128,128]{3,2,1,0:T(8,128)(2,1)S(1)} async-done(((bf16[4,2,128,128]{3,2,1,0:T(8,128)(2,1)}), bf16[4,2,128,128]{3,2,1,0:T(8,128)(2,1)S(1)}, u32[]{:S(2)}, u32[]{:S(2)}) %all-to-all-start) | async-done | bytes 262176 | tf_op jit(solution)/shard_map/all_to_all | solution.py:335
  55.9 0.0 copy-done
  55.9 0.0 copy-done.1
  55.9 0.0 copy-done.2
  55.9 9.5 %formed_and_predicted.1 = (bf16[2,512,512]{2,1,0:T(8,128)(2,1)}, bf16[128,2,128]{2,1,0:T(2,128)(2,1)}) custom-call(s32[64,2]{1,0:T(8,128)S(1)} %copy.25.corner_ref, s32[64]{0:T(128)S(1)} %multiply_add_fusion.target_ref, bf16[4,2,128,128]{3,2,1,0:T(8,128)(2,1)S(1)} %all-to-all-done.mine_ref, bf16[4,512,128]{2,1,0:T(8,128)(2,1)S(1)} %copy-done, ...), custom_call_target="tpu_custom_call" | custom-call | tf_op jit(solution)/shard_map/formed_and_predicted/pallas_call | solution.py:280
  65.4 2.9 %all-to-all-start.1 = ((bf16[32,4,2,128]{3,2,1,0:T(2,128)(2,1)}), bf16[32,4,2,128]{3,2,1,0:T(2,128)(2,1)S(1)}, u32[]{:S(2)}, u32[]{:S(2)}) async-start(bf16[32,4,2,128]{3,2,1,0:T(2,128)(2,1)} %bitcast.12), calls=%async_computation.1 | async-start | bytes 131072 | tf_op jit(solution)/shard_map/all_to_all | solution.py:349
  68.3 3.3 %gain_products.1 = f32[128,2,128]{2,1,0:T(2,128)} custom-call(f32[2,512]{1,0:T(2,128)} %gains_ref.1, s32[128,2,128]{2,1,0:T(2,128)} %index_ref.1), custom_call_target="tpu_custom_call" | custom-call | tf_op jit(solution)/shard_map/gain_products/pallas_call | solution.py:204
  71.6 4.1 %all-to-all-done.1 = bf16[32,4,2,128]{3,2,1,0:T(2,128)(2,1)S(1)} async-done(((bf16[32,4,2,128]{3,2,1,0:T(2,128)(2,1)}), bf16[32,4,2,128]{3,2,1,0:T(2,128)(2,1)S(1)}, u32[]{:S(2)}, u32[]{:S(2)}) %all-to-all-start.1) | async-done | bytes 65568 | tf_op jit(solution)/shard_map/all_to_all | solution.py:349
  75.7 0.0 copy-done.3
  75.7 1.7 %fusion.13 = f32[128,2,128]{2,1,0:T(2,128)} fusion(f32[128,2,128]{2,1,0:T(2,128)S(1)} %copy-done.3, f32[128,2,128]{2,1,0:T(2,128)} %gain_products.1, bf16[32,4,2,128]{3,2,1,0:T(2,128)(2,1)S(1)} %all-to-all-done.1), kind=kLoop, calls=%fused_computation.11 | loop fusion | flops 98304 | bytes 458752 | tf_op jit(solution)/shard_map/sub | solution.py:354
  (7 shorter events, 0.1 us)
Async XLA Ops:
  39.2 6.5 %copy-start.4 = (s32[64,2]{0,1:T(2,128)S(1)}, s32[64,2]{0,1:T(2,128)}, u32[]{:S(2)}) copy-start(s32[64,2]{0,1:T(2,128)} %param.20) | copy-start | bytes 1540
  39.2 6.6 %copy-start.5 = (s32[64,1]{0,1:T(1,128)S(1)}, s32[64,1]{0,1:T(1,128)}, u32[]{:S(2)}) copy-start(s32[64,1]{0,1:T(1,128)} %param.22) | copy-start | bytes 772
  39.3 16.7 %copy-start = (bf16[4,512,128]{2,1,0:T(8,128)(2,1)S(1)}, bf16[4,512,128]{2,1,0:T(8,128)(2,1)}, u32[]{:S(2)}) copy-start(bf16[4,512,128]{2,1,0:T(8,128)(2,1)} %cols_ref.1) | copy-start | bytes 1572868
  39.3 16.7 %copy-start.1 = (bf16[4,512,128]{2,1,0:T(8,128)(2,1)S(1)}, bf16[4,512,128]{2,1,0:T(8,128)(2,1)}, u32[]{:S(2)}) copy-start(bf16[4,512,128]{2,1,0:T(8,128)(2,1)} %rows_ref.1) | copy-start | bytes 1572868
  39.3 16.6 %copy-start.2 = (f32[64,2,128]{2,1,0:T(2,128)S(1)}, f32[64,2,128]{2,1,0:T(2,128)}, u32[]{:S(2)}) copy-start(f32[64,2,128]{2,1,0:T(2,128)} %offset_ref.1) | copy-start | bytes 196612
  39.3 36.4 %copy-start.3 = (f32[128,2,128]{2,1,0:T(2,128)S(1)}, f32[128,2,128]{2,1,0:T(2,128)}, u32[]{:S(2)}) copy-start(f32[128,2,128]{2,1,0:T(2,128)} %param.23) | copy-start | bytes 393220
  40.9 15.0 %all-to-all-start = ((bf16[4,2,128,128]{3,2,1,0:T(8,128)(2,1)}), bf16[4,2,128,128]{3,2,1,0:T(8,128)(2,1)S(1)}, u32[]{:S(2)}, u32[]{:S(2)}) async-start(bf16[4,2,128,128]{3,2,1,0:T(8,128)(2,1)} %broadcast_select_fusion), calls=%async_computation | async-start | bytes 524288 | tf_op jit(solution)/shard_map/all_to_all | solution.py:335
  65.4 10.3 %all-to-all-start.1 = ((bf16[32,4,2,128]{3,2,1,0:T(2,128)(2,1)}), bf16[32,4,2,128]{3,2,1,0:T(2,128)(2,1)S(1)}, u32[]{:S(2)}, u32[]{:S(2)}) async-start(bf16[32,4,2,128]{3,2,1,0:T(2,128)(2,1)} %bitcast.12), calls=%async_computation.1 | async-start | bytes 131072 | tf_op jit(solution)/shard_map/all_to_all | solution.py:349

commit v4 on v3

--- a/solution.py
+++ b/solution.py
@@ -181,6 +181,55 @@
     )(order, kernels, comp, taper)
 
 
+def exchange_kernel(count, order_ref, finished_ref, out_ref, stage_ref, send_sem, recv_sem):
+    corr = finished_ref.shape[0]
+    me = lax.axis_index("facet")
+    barrier = pltpu.get_barrier_semaphore()
+    for off in range(1, count):
+        pl.semaphore_signal(
+            barrier, inc=1, device_id={"facet": lax.rem(me + off, count)}, device_id_type=MESH
+        )
+    for d in range(count):
+        for c in range(corr):
+            stage_ref[d, c] = finished_ref[c, order_ref[d]]
+    pl.semaphore_wait(barrier, count - 1)
+    copies = []
+    for off in range(1, count):
+        peer = lax.rem(me + off, count)
+        copy = pltpu.make_async_remote_copy(
+            src_ref=stage_ref.at[peer],
+            dst_ref=out_ref.at[me],
+            send_sem=send_sem.at[off],
+            recv_sem=recv_sem.at[off],
+            device_id={"facet": peer},
+            device_id_type=MESH,
+        )
+        copy.start()
+        copies.append(copy)
+    out_ref[me] = stage_ref[me]
+    for copy in copies:
+        copy.wait()
+
+
+def exchanged(finished, order):
+    corr, count, rows, cols = finished.shape
+    whole = pl.BlockSpec(memory_space=pltpu.VMEM)
+    shape = (count, corr, rows, cols)
+    return pl.pallas_call(
+        functools.partial(exchange_kernel, count),
+        in_specs=[pl.BlockSpec(memory_space=pltpu.SMEM), whole],
+        out_specs=whole,
+        scratch_shapes=[
+            pltpu.VMEM(shape, finished.dtype),
+            pltpu.SemaphoreType.DMA((count,)),
+            pltpu.SemaphoreType.DMA((count,)),
+        ],
+        out_shape=jax.ShapeDtypeStruct(shape, finished.dtype),
+        compiler_params=pltpu.CompilerParams(collective_id=1, has_side_effects=True),
+        name="exchanged",
+    )(order, finished)
+
+
 def looked_up(row, index):
     low, high = index % LANES, index // LANES
     out = None
@@ -323,16 +372,15 @@
     sub_rows = row_taper.shape[2] // contrib_side
     sub_cols = col_taper.shape[2] // contrib_side
     col_perm = subgrid_owner[:sub_cols] % n_strip
-    row_perm = subgrid_owner[jnp.arange(sub_rows, dtype=jnp.int32) * sub_cols] // n_strip
+    row_perm = subgrid_owner.reshape(sub_rows, sub_cols)[:, 0] // n_strip
     col_inverse = inverse_of(col_perm)
     row_inverse = inverse_of(row_perm)
     regrouped = regrouped_products(comp, scale_kernels, col_taper[0], col_inverse)
-    all_rows = row_taper[0].reshape(n_strip, rows, sub_rows, contrib_side)
+    all_rows = row_taper[0].reshape(n_strip, rows, sub_rows * contrib_side)
     finished = jnp.einsum(
-        "xrai,xcrj->acij", all_rows, regrouped, preferred_element_type=jnp.float32
+        "xrm,xcrj->cmj", all_rows, regrouped, preferred_element_type=jnp.float32
     ).astype(jnp.bfloat16)
-    outgoing = jnp.take(finished, row_inverse, axis=0)
-    mine = lax.all_to_all(outgoing, "facet", split_axis=0, concat_axis=0, tiled=True)
+    mine = exchanged(finished.reshape(corr, sub_rows, contrib_side, contrib_side), row_inverse)
     blocks = block_owner.shape[0]
     visibility_block = observed.shape[2]
     dest = block_owner[:, 0]

time: 77.8 us -> 74.9 us (0.963)
  Pallas kernels: 44 us -> 55.6 us
  waiting for transfers between devices: 14 us -> 4.15 us
  starting transfers between devices: 7.74 us -> 5.34 us
  local copies, waits for them, and re-layouts: 4.76 us -> 2.77 us
    pallas_call x0 -> x1, Pallas kernels: none -> 11.5 us  [exchanged(): pl.pallas_call(functools.partial(exchange_kernel, count), in_specs=[pl.Bl...]
    all_to_all x1 -> x0, waiting for transfers between devices: 9.87 us -> none  [on_device(): lax.all_to_all(outgoing, 'facet', split_axis=0, concat_axis=0, tiled=True)]
    all_to_all x1 -> x0, starting transfers between devices: 4.87 us -> none  [on_device(): lax.all_to_all(outgoing, 'facet', split_axis=0, concat_axis=0, tiled=True)]
    another operation x1 -> x0, local copies, waits for them, and re-layouts: 2.55 us -> none  [on_device(): all_rows = row_taper[0].reshape(n_strip, rows, sub_rows, contrib_side)]
    all_to_all x1, starting transfers between devices: 2.87 us -> 5.34 us  [on_device(): lax.all_to_all(outgoing_vis, ('facet', 'strip'), split_axis=0, concat_axi...]
    gather x2 -> x0, local copies, waits for them, and re-layouts: 1.89 us -> none  [the longest x1 1.29 us: on_device(): subgrid_owner[jnp.arange(sub_rows, dtype=jnp.int32) * sub_cols] // n_strip]
    unnamed x13 -> x17, local copies, waits for them, and re-layouts: 0.13 us -> 1.08 us
    select_n x4 -> x1, other arithmetic: 0.82 us -> 0.01 us  [on_device(): row_perm = subgrid_owner.reshape(sub_rows, sub_cols)[:, 0] // n_strip]
  transfers between devices with their start and end apart: 2 -> 1, of which waited for: 2 -> 1; matrix products, arithmetic and copies ran while one was open for 0% -> 0% of each run, Pallas kernels for 4% -> 4%
where the time goes in v4:
time: 74.9 us; the launch traced here: 74.6 us
  Pallas kernels  55.6 us (74%)
  starting transfers between devices  5.34 us (7%)
  waiting for transfers between devices  4.15 us (6%)
  other arithmetic  3.92 us (5%)
  local copies, waits for them, and re-layouts  2.77 us (4%)
  matrix products  2.03 us (3%)
  between operations  0.76 us (1%)
    pallas_call x1, Pallas kernels, regrouped_products(): pl.pallas_call(functools.partial(smooth_kernel, count), in_specs=[scalars...  31.3 us
    pallas_call x1, Pallas kernels, exchanged(): pl.pallas_call(functools.partial(exchange_kernel, count), in_specs=[pl.Bl...  11.5 us
    pallas_call x1, Pallas kernels, formed_and_predicted(): pl.pallas_call(degrid_kernel, in_specs=[scalars, scalars, whole, whole, w...  9.5 us
    all_to_all x1, starting transfers between devices, on_device(): lax.all_to_all(outgoing_vis, ('facet', 'strip'), split_axis=0, concat_axi...  5.34 us
    all_to_all x1, waiting for transfers between devices, on_device(): lax.all_to_all(outgoing_vis, ('facet', 'strip'), split_axis=0, concat_axi...  4.15 us
    pallas_call x1, Pallas kernels, gain_products(): pl.pallas_call(gain_kernel, grid=(rows // step,), in_specs=[pl.BlockSpec(...  3.26 us
    dot_general x1, matrix products, on_device(): jnp.einsum('xrm,xcrj->cmj', all_rows, regrouped, preferred_element_type=j...  2.03 us
    sub x1, other arithmetic, on_device(): residual = observed - product * placed  1.66 us
  transfers between devices with their start and end apart: 1, of which 1 were waited for; matrix products, arithmetic and copies ran while one was open for 0% of the time, Pallas kernels for 4%

profile of v4, /device:TPU:0, one launch (start us, length us, event | category | flops | bytes accessed | tf_op | source)
XLA Modules:
  0.0 74.6 jit_solution(16543966142662122508)
XLA Ops:
  0.6 0.0 copy-start
  0.6 0.8 %and_select_fusion = s32[8]{0:T(128)S(1)} fusion(s32[32]{0:T(128)} %param.19), kind=kLoop, calls=%fused_computation.15 | loop fusion | flops 88 | bytes 64 | tf_op jit(solution)/shard_map/jit(remainder)/select_n | solution.py:374
  1.5 0.7 reshape.49
  2.2 0.6 select_reduce_fusion.order_ref
  2.8 31.3 %regrouped_products.1 = bf16[8,2,256,128]{3,2,1,0:T(8,128)(2,1)} custom-call(s32[8]{0:T(128)} %select_reduce_fusion.order_ref, f32[4,33]{1,0:T(4,128)} %taps_ref.1, bf16[2,4,256,2048]{3,2,1,0:T(8,128)(2,1)} %bitcast.26, bf16[2048,1024]{1,0:T(8,128)(2,1)} %bitcast.27), custom_call_target="tpu_custom_call" | custom-call | tf_op jit(solution)/shard_map/regrouped_products/pallas_call | solution.py:156
  34.1 0.0 copy-done
  34.2 0.0 copy-start.6
  34.2 0.0 copy-start.7
  34.2 0.0 copy-start.2
  34.2 0.0 copy-start.3
  34.2 0.0 copy-start.4
  34.2 2.0 %fusion.1 = bf16[2,512,128]{1,2,0:T(8,128)(2,1)S(1)} fusion(bf16[8,2,256,128]{3,2,1,0:T(8,128)(2,1)} %regrouped_products.1, bf16[8,256,512,1]{2,1,3,0:T(8,128)(2,1)S(1)} %bitcast.25), kind=kOutput, calls=%fused_computation.2 | convolution fusion | flops 537001984 | bytes 3407872 | tf_op jit(solution)/shard_map/xrm,xcrj->cmj/dot_general | solution.py:380
  36.3 0.8 %copy.22 = bf16[2,512,128]{2,1,0:T(8,128)(2,1)} copy(bf16[2,512,128]{1,2,0:T(8,128)(2,1)S(1)} %fusion.1) | data formatting | bytes 524288 | tf_op jit(solution)/shard_map/convert_element_type | solution.py:382
  37.1 0.0 copy-start.5
  37.1 0.1 slice_reduce_fusion
  37.2 0.6 select_reduce_fusion.1.order_ref
  37.9 0.0 copy-done.6
  37.9 0.1 copy.23.corner_ref
  38.0 0.0 copy-done.7
  38.0 0.2 convert_reduce_fusion
  38.1 11.5 %exchanged.1.mine_ref = bf16[4,2,128,128]{3,2,1,0:T(8,128)(2,1)} custom-call(s32[4]{0:T(128)} %select_reduce_fusion.1.order_ref, bf16[2,4,128,128]{3,2,1,0:T(8,128)(2,1)} %bitcast.28), custom_call_target="tpu_custom_call" | custom-call | tf_op jit(solution)/shard_map/exchanged/pallas_call | solution.py:218
  49.7 0.0 copy-done.2
  49.7 0.0 copy-done.3
  49.7 0.0 copy-done.4
  49.7 0.0 copy-start.1
  49.7 0.9 %copy-done.1 = bf16[4,2,128,128]{3,2,1,0:T(8,128)(2,1)S(1)} copy-done((bf16[4,2,128,128]{3,2,1,0:T(8,128)(2,1)S(1)}, bf16[4,2,128,128]{3,2,1,0:T(8,128)(2,1)}, u32[]{:S(2)}) %copy-start.1) | copy-done | bytes 262168
  50.7 9.5 %formed_and_predicted.1 = (bf16[2,512,512]{2,1,0:T(8,128)(2,1)}, bf16[128,2,128]{2,1,0:T(2,128)(2,1)}) custom-call(s32[64,2]{1,0:T(8,128)S(1)} %copy.23.corner_ref, s32[64]{0:T(128)S(1)} %multiply_add_fusion.target_ref, bf16[4,2,128,128]{3,2,1,0:T(8,128)(2,1)S(1)} %copy-done.1, bf16[4,512,128]{2,1,0:T(8,128)(2,1)S(1)} %copy-done.2, ...), custom_call_target="tpu_custom_call" | custom-call | tf_op jit(solution)/shard_map/formed_and_predicted/pallas_call | solution.py:329
  60.2 5.3 %all-to-all-start = ((bf16[32,4,2,128]{3,2,1,0:T(2,128)(2,1)}), bf16[32,4,2,128]{3,2,1,0:T(2,128)(2,1)S(1)}, u32[]{:S(2)}, u32[]{:S(2)}) async-start(bf16[32,4,2,128]{3,2,1,0:T(2,128)(2,1)} %bitcast.10), calls=%async_computation | async-start | bytes 131072 | tf_op jit(solution)/shard_map/all_to_all | solution.py:397
  65.5 3.3 %gain_products.1 = f32[128,2,128]{2,1,0:T(2,128)} custom-call(f32[2,512]{1,0:T(2,128)} %gains_ref.1, s32[128,2,128]{2,1,0:T(2,128)} %index_ref.1), custom_call_target="tpu_custom_call" | custom-call | tf_op jit(solution)/shard_map/gain_products/pallas_call | solution.py:253
  68.8 4.1 %all-to-all-done = bf16[32,4,2,128]{3,2,1,0:T(2,128)(2,1)S(1)} async-done(((bf16[32,4,2,128]{3,2,1,0:T(2,128)(2,1)}), bf16[32,4,2,128]{3,2,1,0:T(2,128)(2,1)S(1)}, u32[]{:S(2)}, u32[]{:S(2)}) %all-to-all-start) | async-done | bytes 65568 | tf_op jit(solution)/shard_map/all_to_all | solution.py:397
  72.9 0.0 copy-done.5
  72.9 1.7 %fusion.2 = f32[128,2,128]{2,1,0:T(2,128)} fusion(f32[128,2,128]{2,1,0:T(2,128)S(1)} %copy-done.5, f32[128,2,128]{2,1,0:T(2,128)} %gain_products.1, bf16[32,4,2,128]{3,2,1,0:T(2,128)(2,1)S(1)} %all-to-all-done), kind=kLoop, calls=%fused_computation.4 | loop fusion | flops 98304 | bytes 458752 | tf_op jit(solution)/shard_map/sub | solution.py:402
  (2 shorter events, 0.0 us)
Async XLA Ops:
  0.6 33.5 %copy-start = (bf16[1,2048,512]{2,1,0:T(8,128)(2,1)S(1)}, bf16[1,2048,512]{2,1,0:T(8,128)(2,1)}, u32[]{:S(2)}) copy-start(bf16[1,2048,512]{2,1,0:T(8,128)(2,1)} %param.15) | copy-start | bytes 6291460
  34.2 3.7 %copy-start.6 = (s32[64,2]{0,1:T(2,128)S(1)}, s32[64,2]{0,1:T(2,128)}, u32[]{:S(2)}) copy-start(s32[64,2]{0,1:T(2,128)} %param.20) | copy-start | bytes 1540
  34.2 3.8 %copy-start.7 = (s32[64,1]{0,1:T(1,128)S(1)}, s32[64,1]{0,1:T(1,128)}, u32[]{:S(2)}) copy-start(s32[64,1]{0,1:T(1,128)} %param.22) | copy-start | bytes 772
  34.2 15.5 %copy-start.2 = (bf16[4,512,128]{2,1,0:T(8,128)(2,1)S(1)}, bf16[4,512,128]{2,1,0:T(8,128)(2,1)}, u32[]{:S(2)}) copy-start(bf16[4,512,128]{2,1,0:T(8,128)(2,1)} %cols_ref.1) | copy-start | bytes 1572868
  34.2 15.5 %copy-start.3 = (bf16[4,512,128]{2,1,0:T(8,128)(2,1)S(1)}, bf16[4,512,128]{2,1,0:T(8,128)(2,1)}, u32[]{:S(2)}) copy-start(bf16[4,512,128]{2,1,0:T(8,128)(2,1)} %rows_ref.1) | copy-start | bytes 1572868
  34.2 15.5 %copy-start.4 = (f32[64,2,128]{2,1,0:T(2,128)S(1)}, f32[64,2,128]{2,1,0:T(2,128)}, u32[]{:S(2)}) copy-start(f32[64,2,128]{2,1,0:T(2,128)} %offset_ref.1) | copy-start | bytes 196612
  37.1 35.8 %copy-start.5 = (f32[128,2,128]{2,1,0:T(2,128)S(1)}, f32[128,2,128]{2,1,0:T(2,128)}, u32[]{:S(2)}) copy-start(f32[128,2,128]{2,1,0:T(2,128)} %param.23) | copy-start | bytes 393220
  49.7 1.0 %copy-start.1 = (bf16[4,2,128,128]{3,2,1,0:T(8,128)(2,1)S(1)}, bf16[4,2,128,128]{3,2,1,0:T(8,128)(2,1)}, u32[]{:S(2)}) copy-start(bf16[4,2,128,128]{3,2,1,0:T(8,128)(2,1)} %exchanged.1.mine_ref) | copy-start | bytes 786436
  60.2 12.8 %all-to-all-start = ((bf16[32,4,2,128]{3,2,1,0:T(2,128)(2,1)}), bf16[32,4,2,128]{3,2,1,0:T(2,128)(2,1)S(1)}, u32[]{:S(2)}, u32[]{:S(2)}) async-start(bf16[32,4,2,128]{3,2,1,0:T(2,128)(2,1)} %bitcast.10), calls=%async_computation | async-start | bytes 131072 | tf_op jit(solution)/shard_map/all_to_all | solution.py:397
